TPU v7x, 512 devices: a whole 4x8x8 slice. The times are simulated.
512 devices in a mesh: seq: 64 (over y, x, core), fsdp: 8 (over z).
Axes of the slice: x: 4, y: 8, z: 8, core: 2. Of those that a mesh axis runs over, the one named last changes fastest.
Arguments:
- activation_entries: bfloat16 [8192, 4096], P('seq', 'fsdp'), may hold values from -6 to 6
- content_mapping_matrix: bfloat16 [4096, 4096], P('seq', 'fsdp'), may hold values from -0.09375 to 0.09375
- content_lagged_blend: float32 [4096], P('fsdp'), may hold values from 0 to 1
- acceptance_vectors: bfloat16 [8192, 4096], P('seq', 'fsdp'), may hold values from -6 to 6
- address_vectors_given: bfloat16 [8192, 4096], P('seq', 'fsdp'), may hold values from -6 to 6
- inline_adaptation_speed: bfloat16 [8192, 4096], P('seq', 'fsdp'), may hold values from 0 to 1
- memory_fading_factors: float32 [8192, 4096], P('seq', 'fsdp'), may hold values from 0.6 to 1
- result_filter_given: bfloat16 [8192, 4096], P('seq', 'fsdp'), may hold values from 0.099609375 to 1.5
- extra_coordinate_factors: float32 [4096], P('fsdp'), may hold values from -0.75 to 0.75
- group_layernorm_scaling: float32 [4096], P('fsdp'), may hold values from 0.1 to 1.9
- group_layernorm_offset: float32 [4096], P('fsdp'), may hold values from -4 to 4
Outputs:
- time_mix: bfloat16 [8192, 4096], P('seq', 'fsdp')
All inputs are finite; a program needn't handle non-finite values.
Results may differ from a plain program's by a relative error of at most 0.0056.
Values may be sent and summed in bfloat16 or wider, within the bound.
A program may use at most 64 MiB of HBM per device.

v0:
```python
import jax
import jax.numpy as jnp
from jax import lax
from jax.sharding import PartitionSpec as P

GROUP_DIMENSION = 64


norm_eps = 0.00064
unit_eps = 1e-05
highest = lax.Precision.HIGHEST


def shifted_2(value, axis, steps):
    count = lax.axis_size(axis)
    first, last = (max(0, -steps), min(count, count - steps))
    return lax.ppermute(value, axis, [(source, source + steps) for source in range(first, last)])


def prefix_2(value, axis, join, neutral):
    count, mine = (lax.axis_size(axis), lax.axis_index(axis))
    pieces = lax.all_gather(value, axis)
    so_far = jnp.full_like(value, 0) + jnp.asarray(neutral, value.dtype)

    def step(position, so_far):
        longer = join(so_far, pieces[position])
        return jnp.where(position < mine, longer, so_far)

    return lax.fori_loop(0, count - 1, step, so_far)


def shards(
    activation_entries,
    content_mapping_matrix,
    content_lagged_blend,
    acceptance_vectors,
    address_vectors_given,
    inline_adaptation_speed,
    memory_fading_factors,
    result_filter_given,
    extra_coordinate_factors,
    group_layernorm_scaling,
    group_layernorm_offset,
):
    element_matrix_lines, portion_breadth = activation_entries.shape
    resident_groups = portion_breadth // GROUP_DIMENSION
    as_float = activation_entries.astype(jnp.float32)
    previous = shifted_2(activation_entries[-1:, :], "seq", 1)
    shifted = jnp.concatenate([previous.astype(jnp.float32), as_float[:-1]], axis=0)
    mixed = (as_float + (shifted - as_float) * content_lagged_blend[None, :]).astype(jnp.bfloat16)
    columns = lax.all_gather(content_mapping_matrix, "seq", axis=0, tiled=True)
    projected = jnp.dot(
        lax.all_gather(mixed, "fsdp", axis=1, tiled=True),
        columns,
        preferred_element_type=jnp.float32,
    )
    value = projected.astype(jnp.bfloat16)
    block_len = min(128, element_matrix_lines)
    blocks = element_matrix_lines // block_len

    def split_heads(array):
        shaped = array.astype(jnp.float32).reshape(
            blocks, block_len, resident_groups, GROUP_DIMENSION
        )
        return shaped.transpose(0, 2, 1, 3)

    rec_blocks = split_heads(acceptance_vectors)
    key_blocks = split_heads(address_vectors_given)
    rate_blocks = split_heads(inline_adaptation_speed)
    decay_blocks = split_heads(memory_fading_factors)
    value_blocks = split_heads(value)
    unit = key_blocks * lax.rsqrt(
        jnp.sum(key_blocks * key_blocks, axis=-1, keepdims=True) + unit_eps
    )
    cumul = jnp.cumprod(decay_blocks, axis=2)
    cumul_prev = jnp.concatenate([jnp.ones_like(cumul[:, :, :1]), cumul[:, :, :-1]], axis=2)
    cumul_end = cumul[:, :, -1:, :]
    erase_dir = -unit * cumul_prev
    write_dir = unit * rate_blocks / cumul
    key_scaled = key_blocks / cumul
    rec_scaled = rec_blocks * cumul
    strict = jnp.tril(jnp.ones((block_len, block_len), jnp.float32), -1)
    inclusive = jnp.tril(jnp.ones((block_len, block_len), jnp.float32))
    eye_block = jnp.eye(block_len, dtype=jnp.float32)
    erase_write = jnp.einsum("bhck,bhdk->bhcd", erase_dir, write_dir, precision=highest) * strict
    erase_key = jnp.einsum("bhck,bhdk->bhcd", erase_dir, key_scaled, precision=highest) * strict
    read_write = jnp.einsum("bhck,bhdk->bhcd", rec_scaled, write_dir, precision=highest) * inclusive
    read_key = jnp.einsum("bhck,bhdk->bhcd", rec_scaled, key_scaled, precision=highest) * inclusive
    system = eye_block - erase_write
    write_end = write_dir * cumul_end
    key_end = key_scaled * cumul_end

    def run_blocks(initial, values, want_rows):

        def block_step(state, inputs):
            (
                erase_b,
                rec_b,
                system_b,
                erase_key_b,
                read_write_b,
                read_key_b,
                write_e,
                key_e,
                cumul_e,
                value_b,
            ) = inputs
            rhs = jnp.einsum("hck,hrk->hcr", erase_b, state, precision=highest) + jnp.einsum(
                "hcd,hdr->hcr", erase_key_b, value_b, precision=highest
            )
            pseudo = lax.linalg.triangular_solve(
                system_b, rhs, left_side=True, lower=True, unit_diagonal=True
            )
            new_state = (
                state * cumul_e
                + jnp.einsum("hcr,hck->hrk", pseudo, write_e, precision=highest)
                + jnp.einsum("hcr,hck->hrk", value_b, key_e, precision=highest)
            )
            if want_rows:
                out_rows = (
                    jnp.einsum("hck,hrk->hcr", rec_b, state, precision=highest)
                    + jnp.einsum("hcd,hdr->hcr", read_write_b, pseudo, precision=highest)
                    + jnp.einsum("hcd,hdr->hcr", read_key_b, value_b, precision=highest)
                )
                return (new_state, out_rows)
            return (new_state, None)

        inputs = (
            erase_dir,
            rec_scaled,
            system,
            erase_key,
            read_write,
            read_key,
            write_end,
            key_end,
            cumul_end,
            values,
        )
        return lax.scan(block_step, initial, inputs)

    identity_part = jnp.broadcast_to(
        jnp.eye(GROUP_DIMENSION, dtype=jnp.float32),
        (resident_groups, GROUP_DIMENSION, GROUP_DIMENSION),
    )
    zero_part = jnp.zeros((resident_groups, GROUP_DIMENSION, GROUP_DIMENSION), jnp.float32)
    start_aug = jnp.concatenate([zero_part, identity_part], axis=1)
    values_aug = jnp.concatenate([value_blocks, jnp.zeros_like(value_blocks)], axis=-1)
    ends, outs_aug = run_blocks(start_aug, values_aug, False)
    payload = jnp.swapaxes(ends, 1, 2)

    def combine_pairs(earlier, later):
        moved = jnp.einsum(
            "hij,hjr->hir", later[:, :, GROUP_DIMENSION:], earlier, precision=highest
        )
        return moved + jnp.concatenate(
            [later[:, :, :GROUP_DIMENSION], jnp.zeros_like(later[:, :, GROUP_DIMENSION:])], axis=-1
        )

    identity_pair = jnp.concatenate([zero_part, identity_part], axis=-1)
    prefix = prefix_2(payload, "seq", combine_pairs, identity_pair)
    incoming = jnp.swapaxes(prefix[:, :, :GROUP_DIMENSION], 1, 2)
    final_state, read_blocks = run_blocks(incoming, value_blocks, True)
    read = read_blocks.transpose(0, 2, 1, 3).reshape(
        element_matrix_lines, resident_groups, GROUP_DIMENSION
    )
    centre = read - jnp.mean(read, axis=-1, keepdims=True)
    spread = jnp.mean(centre * centre, axis=-1, keepdims=True)
    standardized_result = (centre * lax.rsqrt(spread + norm_eps)).reshape(
        element_matrix_lines, portion_breadth
    ) * group_layernorm_scaling[None, :] + group_layernorm_offset[None, :]
    acceptance_by_group = acceptance_vectors.astype(jnp.float32).reshape(
        element_matrix_lines, resident_groups, GROUP_DIMENSION
    )
    address_by_group = address_vectors_given.astype(jnp.float32).reshape(
        element_matrix_lines, resident_groups, GROUP_DIMENSION
    )
    content_by_group = value.astype(jnp.float32).reshape(
        element_matrix_lines, resident_groups, GROUP_DIMENSION
    )
    scaled_aggregate_figure = jnp.sum(
        acceptance_by_group
        * address_by_group
        * extra_coordinate_factors.reshape(resident_groups, GROUP_DIMENSION)[None],
        axis=-1,
        keepdims=True,
    )
    present_extra_term = (scaled_aggregate_figure * content_by_group).reshape(
        element_matrix_lines, portion_breadth
    )
    return (
        (standardized_result + present_extra_term) * result_filter_given.astype(jnp.float32)
    ).astype(jnp.bfloat16)


def solution(mesh):
    return jax.shard_map(
        shards,
        mesh=mesh,
        in_specs=(
            P("seq", "fsdp"),
            P("seq", "fsdp"),
            P("fsdp"),
            P("seq", "fsdp"),
            P("seq", "fsdp"),
            P("seq", "fsdp"),
            P("seq", "fsdp"),
            P("seq", "fsdp"),
            P("fsdp"),
            P("fsdp"),
            P("fsdp"),
        ),
        out_specs=P("seq", "fsdp"),
        check_vma=False,
    )
```

profile of v0, /device:TPU:57, one launch (start us, length us, event | category | flops | bytes accessed | tf_op | source)
XLA Modules:
  0.0 367.6 jit_solution(16223546304854679737)
XLA Ops:
  7.2 3.7 collective-permute-start
  11.9 1.6 fusion.25
  14.3 1.0 copy.54
  15.4 1.1 copy.50
  16.5 1.1 copy.52
  17.8 1.0 copy.56
  19.3 23.3 %fusion.43 = f32[1,8,128,64]{3,1,2,0:T(8,128)S(1)} fusion(f32[1,8,128,64]{3,1,2,0:T(8,128)S(1)} %copy.53), kind=kOutput, calls=%fused_computation.81 | output fusion | flops 8323072 | bytes 524288 | tf_op jit(solution)/shard_map/jit(cumprod)/reduce_window | solution.py:75
  43.8 2.7 multiply_bitcast_fusion.1
  46.5 1.2 copy.58
  47.8 1.2 copy.62
  49.0 1.2 copy.59
  50.4 1.0 fusion.6
  51.4 79.2 %custom-call.7 = f32[8,1,128,128]{2,3,1,0:T(8,128)} custom-call(f32[8,1,128,128]{3,2,1,0:T(8,128)S(1)} %fusion.6), custom_call_target="InvertDiagBlocksLowerTriangular" | custom-call | tf_op jit(solution)/shard_map/while/body/eval_jaxpr/triangular_solve | solution.py:111
  131.3 1.9 fusion.21
  133.3 1.0 convolution_multiply_fusion.2
  134.3 12.5 %all-gather.7.cloned.1.call-done = bf16[4096,512]{1,0:T(8,128)(2,1)} async-done(((bf16[64,512]{1,0:T(8,128)(2,1)}), bf16[4096,512]{1,0:T(8,128)(2,1)}) %all-gather.7.cloned.1.call-update) | async-done | bytes 4194320 | tf_op jit(solution)/shard_map/all_gather | solution.py:51
  146.8 3.2 convolution_convert_fusion
  150.9 1.1 copy.64
  152.1 1.7 convolution_add_fusion.1
  153.8 2.1 fusion.12
  155.8 1.1 convolution_add_fusion.6
  156.9 1.7 fusion.7
  161.4 1.2 copy.70
  162.8 1.0 convolution_multiply_fusion.1
  163.8 1.0 convolution_multiply_fusion
  165.6 95.9 %all-gather.9.cloned.1.call-done = f32[512,64,128]{2,1,0:T(8,128)} async-done(((f32[8,64,128]{2,1,0:T(8,128)}), f32[512,64,128]{2,1,0:T(8,128)}) %all-gather.9.cloned.1.call-update) | async-done | bytes 16777232 | tf_op jit(solution)/shard_map/all_gather | solution.py:22
  261.5 93.2 %while.8 = (s32[]{:T(128)}, f32[8,64,128]{2,1,0:T(8,128)S(1)}, s32[]{:T(128)}, f32[64,8,64,128]{3,2,1,0:T(8,128)}, s32[]{:T(128)}, /*index=5*/pred[128]{0:T(512)(128)(4,1)S(1)}) while((s32[]{:T(128)}, f32[8,64,128]{2,1,0:T(8,128)S(1)}, s32[]{:T(128)}, f32[64,8,64,128]{3,2,1,0:T(8,128)}, s32[]{:T(128)}, ...), condition=%wide.region_3.4_spmd, body=%wide.region_2.3_spmd.sunk | while | flops 50528256 | bytes 2359899 | solution.py:29
  261.5 1.0 dynamic-slice_bitcast_fusion.2
  263.0 1.0 dynamic-slice_bitcast_fusion.2
  264.5 1.0 dynamic-slice_bitcast_fusion.2
  266.0 1.0 dynamic-slice_bitcast_fusion.2
  267.5 1.0 dynamic-slice_bitcast_fusion.2
  270.4 1.0 dynamic-slice_bitcast_fusion.2
  271.9 1.0 dynamic-slice_bitcast_fusion.2
  273.4 1.0 dynamic-slice_bitcast_fusion.2
  274.9 1.0 dynamic-slice_bitcast_fusion.2
  276.3 1.0 dynamic-slice_bitcast_fusion.2
  277.8 1.0 dynamic-slice_bitcast_fusion.2
  279.3 1.0 dynamic-slice_bitcast_fusion.2
  282.3 1.0 dynamic-slice_bitcast_fusion.2
  283.7 1.0 dynamic-slice_bitcast_fusion.2
  285.2 1.0 dynamic-slice_bitcast_fusion.2
  286.7 1.0 dynamic-slice_bitcast_fusion.2
  288.2 1.0 dynamic-slice_bitcast_fusion.2
  289.7 1.0 dynamic-slice_bitcast_fusion.2
  291.1 1.0 dynamic-slice_bitcast_fusion.2
  292.6 1.0 dynamic-slice_bitcast_fusion.2
  294.1 1.0 dynamic-slice_bitcast_fusion.2
  295.6 1.0 dynamic-slice_bitcast_fusion.2
  297.0 1.0 dynamic-slice_bitcast_fusion.2
  298.5 1.0 dynamic-slice_bitcast_fusion.2
  301.5 1.0 dynamic-slice_bitcast_fusion.2
  303.0 1.0 dynamic-slice_bitcast_fusion.2
  304.4 1.0 dynamic-slice_bitcast_fusion.2
  305.9 1.0 dynamic-slice_bitcast_fusion.2
  307.4 1.0 dynamic-slice_bitcast_fusion.2
  308.9 1.0 dynamic-slice_bitcast_fusion.2
  310.4 1.0 dynamic-slice_bitcast_fusion.2
  313.3 1.0 dynamic-slice_bitcast_fusion.2
  314.8 1.0 dynamic-slice_bitcast_fusion.2
  316.3 1.0 dynamic-slice_bitcast_fusion.2
  317.8 1.0 dynamic-slice_bitcast_fusion.2
  355.7 1.6 convolution_add_fusion.4
  357.9 1.1 convolution_add_fusion.3
  (229 shorter events, 69.7 us)
Async XLA Ops:
  6.5 127.8 %all-gather.5.cloned.1.call-start = ((), (), s32[]{:S(2)}) async-start(), calls=%async_computation | async-start | bytes 1179648 | tf_op jit(solution)/shard_map/all_gather | solution.py:53
  7.2 4.6 %collective-permute-start = (bf16[1,512]{1,0:T(2,128)(2,1)S(1)}, bf16[1,512]{1,0:T(2,128)(2,1)S(1)}, u32[]{:S(2)}, u32[]{:S(2)}) collective-permute-start(bf16[1,512]{1,0:T(2,128)(2,1)S(1)} %slice.40), channel_id=1, source_target_pairs={{0,8},{8,16},{16,24},{24,32},{32,40},{40,48},{48,56},{56,64},{64,7... | collective-permute-start | bytes 3080 | tf_op jit(solution)/shard_map/ppermute | solution.py:17
  13.5 133.3 %all-gather.7.cloned.1.call-start = ((), (), s32[]{:S(2)}) async-start(), calls=%async_computation.1 | async-start | bytes 4259840 | tf_op jit(solution)/shard_map/all_gather | solution.py:51
  14.3 247.2 %all-gather.9.cloned.1.call-start = ((), (), s32[]{:S(2)}) async-start(), calls=%async_computation.2 | async-start | bytes 17039360 | tf_op jit(solution)/shard_map/all_gather | solution.py:22
  15.4 31.1 %copy-start.2 = (bf16[128,512]{0,1:T(8,128)(2,1)}, bf16[128,512]{0,1:T(8,128)(2,1)S(1)}, u32[]{:S(2)}) copy-start(bf16[128,512]{0,1:T(8,128)(2,1)S(1)} %copy.54) | copy-start | bytes 393220
  16.5 30.1 %copy-start.4 = (bf16[128,512]{0,1:T(8,128)(2,1)}, bf16[128,512]{0,1:T(8,128)(2,1)S(1)}, u32[]{:S(2)}) copy-start(bf16[128,512]{0,1:T(8,128)(2,1)S(1)} %copy.50) | copy-start | bytes 393220
  130.7 0.6 copy-start.7
  150.1 9.4 %copy-start.12 = (f32[512]{0:T(512)S(1)}, f32[512]{0:T(512)}, u32[]{:S(2)}) copy-start(f32[512]{0:T(512)} %param.21) | copy-start | bytes 6148
  150.1 9.5 %copy-start.3 = (bf16[128,512]{0,1:T(8,128)(2,1)S(1)}, bf16[128,512]{0,1:T(8,128)(2,1)}, u32[]{:S(2)}) copy-start(bf16[128,512]{0,1:T(8,128)(2,1)} %copy-done.2) | copy-start | bytes 393220
  150.1 9.5 %copy-start.5 = (bf16[128,512]{0,1:T(8,128)(2,1)S(1)}, bf16[128,512]{0,1:T(8,128)(2,1)}, u32[]{:S(2)}) copy-start(bf16[128,512]{0,1:T(8,128)(2,1)} %copy-done.4) | copy-start | bytes 393220
  156.9 104.6 %copy-start.9 = (pred[128]{0:T(512)(128)(4,1)S(1)}, pred[128]{0:T(512)(128)(4,1)}, u32[]{:S(2)}) copy-start(pred[128]{0:T(512)(128)(4,1)} %constant.95.clone.1) | copy-start | bytes 388
  261.5 95.8 %copy-start = (f32[8,1,128,128]{2,3,1,0:T(8,128)S(1)}, f32[8,1,128,128]{2,3,1,0:T(8,128)}, u32[]{:S(2)}) copy-start(f32[8,1,128,128]{2,3,1,0:T(8,128)} %custom-call.7) | copy-start | bytes 1572868
  354.9 4.1 %copy-start.1 = (bf16[128,512]{0,1:T(8,128)(2,1)S(1)}, bf16[128,512]{0,1:T(8,128)(2,1)}, u32[]{:S(2)}) copy-start(bf16[128,512]{0,1:T(8,128)(2,1)} %copy.74) | copy-start | bytes 393220
  354.9 5.3 %copy-start.10 = (f32[512]{0:T(512)S(1)}, f32[512]{0:T(512)}, u32[]{:S(2)}) copy-start(f32[512]{0:T(512)} %param.23) | copy-start | bytes 6148
  354.9 5.3 %copy-start.11 = (f32[512]{0:T(512)S(1)}, f32[512]{0:T(512)}, u32[]{:S(2)}) copy-start(f32[512]{0:T(512)} %param.22) | copy-start | bytes 6148
  355.7 4.6 %copy-start.6 = (f32[128,512]{1,0:T(8,128)S(1)}, f32[128,512]{1,0:T(8,128)}, u32[]{:S(2)}) copy-start(f32[128,512]{1,0:T(8,128)} %copy.81) | copy-start | bytes 786436
  357.3 2.9 copy-start.8
Sparse Core Ops, SparseCore 0:
  13.7 42.7 all-gather.4
  59.8 86.9 all-gather.6
  158.8 102.6 all-gather.8
where the time goes:
time: 373 us; the launch traced here: 368 us
  waiting for transfers between devices  109 us (29%)
  other arithmetic  109 us (29%)
  local copies, waits for them, and re-layouts  81 us (22%)
  matrix products  48.5 us (13%)
  between operations  13.7 us (4%)
  starting transfers between devices  3.75 us (1%)
    all_gather x1, waiting for transfers between devices, prefix_2(): pieces = lax.all_gather(value, axis)  95.9 us
    another operation x4, other arithmetic, block_step(): lax.linalg.triangular_solve(system_b, rhs, left_side=True, lower=True, un...  79.3 us
    squeeze x63, local copies, waits for them, and re-layouts, step(): longer = join(so_far, pieces[position])  61.5 us
    dot_general x63, matrix products, combine_pairs(): jnp.einsum('hij,hjr->hir', later[:, :, GROUP_DIMENSION:], earlier, precis...  28.1 us
    another operation x1, other arithmetic, shards(): cumul = jnp.cumprod(decay_blocks, axis=2)  23.3 us
    all_gather x1, waiting for transfers between devices, shards(): columns = lax.all_gather(content_mapping_matrix, 'seq', axis=0, tiled=True)  12.5 us
  transfers between devices with their start and end apart: 4, of which 2 were waited for; matrix products, arithmetic and copies ran while one was open for 35% of the time, Pallas kernels for 0%

commit v1 on v0

v1 whole, which is shorter than its diff:
```python
import functools

import jax
import jax.numpy as jnp
from jax import lax
from jax.experimental import pallas as pl
from jax.experimental.pallas import tpu as pltpu
from jax.sharding import PartitionSpec as P

MESH = pl.DeviceIdType.MESH
F32 = jnp.float32
BF16 = jnp.bfloat16
HEAD = 64
HEADS = 8
TOKENS = 128
WIDTH = HEAD * HEADS
NX, NY, NZ = 4, 8, 8
ROW = 2 * NX
NORM_EPS = 0.00064
UNIT_EPS = 1e-05


def split(x):
    high = x.astype(BF16)
    return high, (x - high.astype(F32)).astype(BF16)


def cat(*parts, axis):
    return jnp.concatenate(parts, axis=axis)


def dot(a, b):
    return jnp.dot(a, b, preferred_element_type=F32)


def dot_nt(a, b):
    return lax.dot_general(a, b, (((1,), (1,)), ((), ())), preferred_element_type=F32)


def wide_left(high, low):
    return cat(high, low, high, axis=1)


def wide_right(high, low):
    return cat(high, high, low, axis=0)


def iota(shape, dim):
    return lax.broadcasted_iota(jnp.int32, shape, dim)


def head_sums(x):
    ones = ((iota((256, 256), 0) // HEAD) == (iota((256, 256), 1) // HEAD)).astype(BF16)
    high, low = split(x)
    sums = dot(cat(high[:, :256], high[:, 256:], axis=0), ones) + dot(
        cat(low[:, :256], low[:, 256:], axis=0), ones
    )
    return cat(sums[:TOKENS], sums[TOKENS:], axis=1)


def shift_rows(x, steps, fill):
    rows = iota(x.shape, 0)
    return jnp.where(rows < steps, fill, pltpu.roll(x, steps, 0))


def prepare(r_ref, k_ref, a_ref, w_ref, bonus_ref, y_ref, q_ref, h_ref, g_ref, coef_ref):
    r = r_ref[...].astype(F32)
    k = k_ref[...].astype(F32)
    a = a_ref[...].astype(F32)
    unit = k * lax.rsqrt(head_sums(k * k) + UNIT_EPS)
    coef_ref[...] = head_sums(r * k * bonus_ref[...])
    cumul = w_ref[...]
    for level in range(7):
        cumul = cumul * shift_rows(cumul, 1 << level, 1.0)
    before = shift_rows(cumul, 1, 1.0)
    inverse = 1.0 / cumul
    end = cumul[TOKENS - 1 :, :]
    erase = -unit * before
    write = unit * a * inverse
    key = k * inverse
    rec = r * cumul
    erase_h, erase_l = split(erase)
    write_h, write_l = split(write)
    key_h, key_l = split(key)
    rec_h, rec_l = split(rec)
    write_end = write * end
    key_end = key * end
    rows, cols = iota((TOKENS, TOKENS), 0), iota((TOKENS, TOKENS), 1)
    strict, inclusive = rows > cols, rows >= cols
    differ = rows ^ cols
    eye = (rows == cols).astype(F32)
    small_eye = iota((HEAD, HEAD), 0) == iota((HEAD, HEAD), 1)

    grams, solves = [], []
    for h in range(HEADS):
        at = slice(HEAD * h, HEAD * (h + 1))
        left = wide_left(
            cat(erase_h[:, at], rec_h[:, at], axis=0), cat(erase_l[:, at], rec_l[:, at], axis=0)
        )
        right = wide_left(
            cat(write_h[:, at], key_h[:, at], axis=0), cat(write_l[:, at], key_l[:, at], axis=0)
        )
        right = cat(right[:, :HEAD], right[:, :HEAD], right[:, HEAD : 2 * HEAD], axis=1)
        grams.append(dot_nt(left, right))
    systems = [jnp.where(strict, gram[:TOKENS, :TOKENS], 0.0) for gram in grams]
    halves = [split(system) for system in systems]
    for h in range(HEADS):
        solves.append(eye + jnp.where(differ == 1, systems[h], 0.0))
    for level in range(1, 7):
        mask = (differ >> level) == 1
        for h in range(HEADS):
            rough = solves[h].astype(BF16)
            part = jnp.where(mask, halves[h][0], jnp.zeros_like(halves[h][0]))
            solves[h] = solves[h] + dot(rough, dot(part, rough).astype(BF16))
    for h in range(HEADS):
        high, low = split(solves[h])
        left_over = eye - solves[h] + dot(wide_left(*halves[h]), wide_right(high, low))
        solves[h] = solves[h] + dot(high, left_over.astype(BF16))
    for pair in range(HEADS // 2):
        wide = slice(2 * HEAD * pair, 2 * HEAD * (pair + 1))
        write_t = write_end[:, wide].T
        key_t = key_end[:, wide].T
        for half in range(2):
            h = 2 * pair + half
            at = slice(HEAD * h, HEAD * (h + 1))
            gram = grams[h]
            erase_key = split(jnp.where(strict, gram[:TOKENS, TOKENS:], 0.0))
            read_write = jnp.where(inclusive, gram[TOKENS:, :TOKENS], 0.0)
            read_key = jnp.where(inclusive, gram[TOKENS:, TOKENS:], 0.0)
            both = dot(
                wide_left(*split(solves[h])),
                wide_right(
                    cat(erase_key[0], erase_h[:, at], axis=1),
                    cat(erase_key[1], erase_l[:, at], axis=1),
                ),
            )
            mine = slice(HEAD * half, HEAD * (half + 1))
            out = dot(
                wide_left(*split(cat(read_write, write_t[mine], axis=0))),
                wide_right(*split(both)),
            )
            y_ref[h] = cat(*split(read_key + out[:TOKENS, :TOKENS]), axis=1)
            q_ref[h] = cat(*split(rec[:, at] + out[:TOKENS, TOKENS:]), axis=1)
            h_ref[h] = cat(*split(key_t[mine] + out[TOKENS:, :TOKENS]), axis=1)
            diagonal = jnp.where(small_eye, end[:, at], 0.0)
            g_ref[h] = cat(*split(diagonal + out[TOKENS:, TOKENS:]), axis=1)


PREPARED = (
    ((HEADS, TOKENS, 2 * TOKENS), BF16),
    ((HEADS, TOKENS, 2 * HEAD), BF16),
    ((HEADS, HEAD, 2 * TOKENS), BF16),
    ((HEADS, HEAD, 2 * HEAD), BF16),
    ((TOKENS, WIDTH), F32),
)


def chain_step(g, z):
    high, low = split(z)
    return dot(cat(g, g[:, :HEAD], axis=1), wide_right(high, low))


def fold(x):
    return x[:, :HEAD] + x[:, HEAD:]


def pack(x):
    return cat(*split(x), axis=1)


def exchange(
    x_ref, w_ref, blend_ref, y_ref, q_ref, h_ref, g_ref, coef_ref, gate_ref, scale_ref, offset_ref,
    out_ref,
    prev_buf, x_send, xg, wa, wb, p_send, p_recv,
    g_row, g_col, z_chain, z_all, z_row,
    l_send, l_row, t_send, t_col, s_send, s_in,
    send, recv, local,
):
    s, z = lax.axis_index("seq"), lax.axis_index("fsdp")
    count = NX * NY * 2
    core, x, y, place = s % 2, (s // 2) % NX, s // ROW, s % ROW
    counter = iter(range(10**6))
    waiting, conditional = [], []

    def at_seq(index):
        return {"seq": index}

    def chip(yy, xx):
        return at_seq((yy * NX + xx) * 2 + core)

    def copy_to(source, target, device):
        n = next(counter)
        copy = pltpu.make_async_remote_copy(
            src_ref=source, dst_ref=target, send_sem=send.at[n], recv_sem=recv.at[n],
            device_id=device, device_id_type=MESH,
        )
        copy.start()
        entry = [copy, False]
        waiting.append(entry)
        return entry

    def arrived(entry):
        if not entry[1]:
            entry[1] = True
            entry[0].wait_recv()

    own_a = pltpu.make_async_copy(w_ref.at[:, pl.ds(0, 256)], wa.at[y, x], local.at[0])
    own_b = pltpu.make_async_copy(w_ref.at[:, pl.ds(256, 256)], wb.at[y, x], local.at[1])
    own_a.start()
    own_b.start()
    for d in range(NY):
        t_col[d] = jnp.zeros((HEAD, 2 * HEAD), BF16)
    barrier = pltpu.get_barrier_semaphore()
    partners = [at_seq(y * ROW + (place + d) % ROW) for d in range(1, ROW)]
    partners += [chip((y + d) % NY, x) for d in range(1, NY)]
    partners += [{"fsdp": (z + 1) % NZ}, {"fsdp": (z + NZ - 1) % NZ}]
    partners += [at_seq((s + 1) % count), at_seq((s + count - 1) % count)]
    for partner in partners:
        pl.semaphore_signal(barrier, inc=1, device_id=partner, device_id_type=MESH)
    pl.semaphore_wait(barrier, len(partners))
    own_a.wait()
    own_b.wait()

    right, left = (x + 1) % NX, (x + NX - 1) % NX
    sides = (1, -1)

    prev = copy_to(x_ref.at[pl.ds(TOKENS - 16, 16)], prev_buf, at_seq((s + 1) % count))
    a_in = [copy_to(wa.at[y, x], wa.at[y, x], chip(y, (x + d) % NX)) for d in range(1, NX)]

    yb = {}
    xb = {}

    def row_at(offset):
        return (y + offset + NY) % NY

    def send_yb(step):
        for side in sides:
            if step > 1:
                arrived(yb[side, step - 1])
            if step == NY // 2 and side < 0:
                continue
            row = row_at(-side * (step - 1))
            yb[side, step] = copy_to(wb.at[row, x], wb.at[row, x], chip(row_at(side), x))

    def send_xb(offset):
        row = row_at(offset)
        for side, to in ((1, right), (-1, left)):
            xb[side, offset] = copy_to(wb.at[row, x], wb.at[row, x], chip(y, to))

    def forward_xb(offset):
        row = row_at(offset)
        if offset % 2 == 0:
            arrived(xb[1, offset])
            copy_to(wb.at[row, left], wb.at[row, left], chip(y, right))
        else:
            arrived(xb[-1, offset])
            copy_to(wb.at[row, right], wb.at[row, right], chip(y, left))

    send_yb(1)
    send_xb(0)

    arrived(prev)
    own = x_ref[...].astype(F32)
    before = jnp.where(s == 0, 0.0, prev_buf[...].astype(F32)[15:16, :])
    shifted = jnp.where(iota((TOKENS, WIDTH), 0) == 0, before, pltpu.roll(own, 1, 0))
    mixed = own + (shifted - own) * blend_ref[...]
    even = cat(*[mixed[:, 128 * q : 128 * q + 64] for q in range(4)], axis=1).astype(BF16)
    odd = cat(*[mixed[:, 128 * q + 64 : 128 * q + 128] for q in range(4)], axis=1).astype(BF16)
    is_even = core == 0
    xg[z, core] = jnp.where(is_even, even, odd)
    x_send[...] = jnp.where(is_even, odd, even)
    mate = at_seq(s + 1 - 2 * core)
    mate_x = copy_to(x_send, xg.at[z, core], mate)

    zx, ya = {}, {}

    def send_zx(step, sub):
        part = core if sub == 0 else 1 - core
        for side in sides:
            if step == NZ // 2 and side != sides[sub]:
                continue
            if step > 1:
                arrived(zx[side, step - 1, sub])
            block = (z + NZ - side * (step - 1)) % NZ
            zx[side, step, sub] = copy_to(
                xg.at[block, part], xg.at[block, part], {"fsdp": (z + NZ + side) % NZ}
            )

    def send_ya(step, sub):
        for side in sides:
            if step == NY // 2 and side != sides[sub]:
                continue
            if step > 1:
                arrived(ya[side, step - 1, sub])
            row = row_at(-side * (step - 1))
            part = wa.at[row, pl.ds(2 * sub, 2)]
            ya[side, step, sub] = copy_to(part, part, chip(row_at(side), x))

    send_zx(1, 0)
    for entry in a_in:
        arrived(entry)
    send_ya(1, 0)
    send_ya(1, 1)
    arrived(mate_x)
    send_zx(1, 1)

    g_in = []
    g_row[place] = g_ref[place]
    for d in range(1, ROW):
        to = (place + d) % ROW
        g_in.append(copy_to(g_ref.at[to], g_row.at[place], at_seq(y * ROW + to)))

    def round_of(step):
        for sub in range(2):
            send_ya(step, sub)
            send_zx(step, sub)
            if sub == 0:
                send_yb(step)
                for offset in (-(step - 1), step - 1):
                    send_xb(offset)
            else:
                if step == 2:
                    forward_xb(0)
                else:
                    for offset in (-(step - 2), step - 2):
                        forward_xb(offset)

    def row_chain():
        for entry in g_in:
            arrived(entry)
        wide = z_chain.shape[1]
        lane, line = iota((HEAD, wide), 1), iota((HEAD, wide), 0)
        chain = (lane == line + ROW * HEAD).astype(F32)
        for j in range(ROW):
            z_all[j] = cat(*split(chain), axis=1)
            chain = chain_step(g_row[j], chain) + (lane == line + j * HEAD).astype(F32)
        z_chain[...] = chain

    def send_g_col():
        total = pack(z_chain[...][:, ROW * HEAD : (ROW + 1) * HEAD])
        g_col[y] = total
        for d in range(1, NY):
            n = next(counter)
            conditional.append(
                (d, n, pltpu.make_async_remote_copy(
                    src_ref=g_col.at[y], dst_ref=g_col.at[y], send_sem=send.at[n], recv_sem=recv.at[n],
                    device_id=chip((y + d) % NY, x), device_id_type=MESH,
                ))
            )

            @pl.when(y + d < NY)
            def _(copy=conditional[-1][2]):
                copy.start()

    def column_chain():
        for d, _, copy in conditional[: NY - 1]:

            @pl.when(y >= d)
            def _(copy=copy):
                copy.wait_recv()

        lane, line = iota((HEAD, NY * HEAD), 1), iota((HEAD, NY * HEAD), 0)
        chain = jnp.zeros((HEAD, NY * HEAD), F32)
        for q in range(NY - 1):
            longer = chain_step(g_col[q], chain) + (lane == line + q * HEAD).astype(F32)
            chain = jnp.where(q < y, longer, chain)
        z_row[...] = cat(*split(chain), axis=0)

    round_of(2)
    row_chain()
    round_of(3)
    send_g_col()
    round_of(4)
    column_chain()
    arrived(yb[1, NY // 2])
    send_xb(-4)
    forward_xb(-3)
    forward_xb(3)
    forward_xb(-4)
    for entry in waiting:
        arrived(entry)

    parts = {}
    for mine in (False, True):
        block = core if mine else 1 - core
        for half, weights in enumerate((wa, wb)):
            total = jnp.zeros((TOKENS, 256), F32)
            for row in range(NY):
                total = total + dot(xg[row, block], weights[row].reshape(256, 256))
            if mine:
                parts[half] = total
            else:
                p_send[half] = total
                parts[half, "copy"] = copy_to(p_send.at[half], p_recv.at[half], mate)
    values = []
    for half in range(2):
        arrived(parts[half, "copy"])
        values.append((parts[half] + p_recv[half]).astype(BF16))
    value = cat(*values, axis=1)

    doubled = []
    for h in range(HEADS):
        v = value[:, HEAD * h : HEAD * (h + 1)]
        doubled.append(cat(v, v, axis=0))
        l_send[h] = pack(dot(h_ref[h], doubled[h]))
    l_in = []
    for d in range(1, ROW):
        to = (place + d) % ROW
        l_in.append(copy_to(l_send.at[to], l_row.at[place], at_seq(y * ROW + to)))
    l_row[place] = l_send[place]
    chain = z_chain[...][:, : ROW * HEAD]
    row_total = cat(*split(chain), axis=0)
    for entry in l_in:
        arrived(entry)
    lows = l_row[...].reshape(ROW * HEAD, 2 * HEAD)
    total = fold(dot(row_total, lows))
    t_send[...] = pack(total[:HEAD] + total[HEAD:])
    first = len(conditional)
    for d in range(1, NY):
        n = next(counter)
        conditional.append(
            (d, n, pltpu.make_async_remote_copy(
                src_ref=t_send, dst_ref=t_col.at[y], send_sem=send.at[n], recv_sem=recv.at[n],
                device_id=chip((y + d) % NY, x), device_id_type=MESH,
            ))
        )

        @pl.when(y + d < NY)
        def _(copy=conditional[-1][2]):
            copy.start()

    wide = ROW * HEAD
    span = z_all.shape[2] // 2
    from_row = []
    for j in range(ROW):
        both = cat(z_all[j, :, :wide], z_all[j, :, span : span + wide], axis=1)
        from_row.append(dot(both, cat(lows, lows, axis=0)))
    reads = [dot(y_ref[h], doubled[h]) for h in range(HEADS)]
    extra = coef_ref[...] * value.astype(F32)
    gate = gate_ref[...].astype(F32)

    for d, _, copy in conditional[first:]:

        @pl.when(y >= d)
        def _(copy=copy):
            copy.wait_recv()

    entering = fold(dot(z_row[...], t_col[...].reshape(NY * HEAD, 2 * HEAD)))
    entering = pack(entering[:HEAD] + entering[HEAD:])
    twice = cat(entering, entering, axis=0)
    for j in range(ROW):
        both = cat(
            z_all[j, :, wide : wide + HEAD], z_all[j, :, span + wide : span + wide + HEAD], axis=1
        )
        s_send[j] = pack(fold(from_row[j] + dot(both, twice)))
    s_wait = []
    for d in range(1, ROW):
        to = (place + d) % ROW
        s_wait.append(copy_to(s_send.at[to], s_in.at[place], at_seq(y * ROW + to)))
    s_in[place] = s_send[place]
    for entry in s_wait:
        arrived(entry)
    for h in range(HEADS):
        state = s_in[h]
        reads[h] = reads[h] + fold(dot(q_ref[h], cat(state, state, axis=0)))
    read = cat(*reads, axis=1)
    centre = read - head_sums(read) * (1.0 / HEAD)
    spread = head_sums(centre * centre) * (1.0 / HEAD)
    normed = centre * lax.rsqrt(spread + NORM_EPS) * scale_ref[...] + offset_ref[...]
    out_ref[...] = ((normed + extra) * gate).astype(BF16)

    for entry in waiting:
        entry[0].wait_send()
    for d, _, copy in conditional:

        @pl.when(y + d < NY)
        def _(copy=copy):
            copy.wait_send()


COPIES = 128
SCRATCH = (
    pltpu.VMEM((16, WIDTH), BF16),
    pltpu.VMEM((TOKENS, 256), BF16),
    pltpu.VMEM((NZ, 2, TOKENS, 256), BF16),
    pltpu.VMEM((NY, NX, HEAD, 256), BF16),
    pltpu.VMEM((NY, NX, HEAD, 256), BF16),
    pltpu.VMEM((2, TOKENS, 256), F32),
    pltpu.VMEM((2, TOKENS, 256), F32),
    pltpu.VMEM((ROW, HEAD, 2 * HEAD), BF16),
    pltpu.VMEM((NY, HEAD, 2 * HEAD), BF16),
    pltpu.VMEM((HEAD, 640), F32),
    pltpu.VMEM((ROW, HEAD, 2 * 640), BF16),
    pltpu.VMEM((2 * HEAD, NY * HEAD), BF16),
    pltpu.VMEM((HEADS, HEAD, 2 * HEAD), BF16),
    pltpu.VMEM((ROW, HEAD, 2 * HEAD), BF16),
    pltpu.VMEM((HEAD, 2 * HEAD), BF16),
    pltpu.VMEM((NY, HEAD, 2 * HEAD), BF16),
    pltpu.VMEM((ROW, HEAD, 2 * HEAD), BF16),
    pltpu.VMEM((HEADS, HEAD, 2 * HEAD), BF16),
    pltpu.SemaphoreType.DMA((COPIES,)),
    pltpu.SemaphoreType.DMA((COPIES,)),
    pltpu.SemaphoreType.DMA((2,)),
)


def shards(
    activation_entries,
    content_mapping_matrix,
    content_lagged_blend,
    acceptance_vectors,
    address_vectors_given,
    inline_adaptation_speed,
    memory_fading_factors,
    result_filter_given,
    extra_coordinate_factors,
    group_layernorm_scaling,
    group_layernorm_offset,
):
    vmem = pl.BlockSpec(memory_space=pltpu.VMEM)

    def row(vector):
        return vector.reshape(1, WIDTH)

    prepared = pl.pallas_call(
        prepare,
        out_shape=[jax.ShapeDtypeStruct(shape, kind) for shape, kind in PREPARED],
        in_specs=[vmem] * 5,
        out_specs=[vmem] * len(PREPARED),
        compiler_params=pltpu.CompilerParams(vmem_limit_bytes=56 << 20),
        name="prepare",
    )(
        acceptance_vectors,
        address_vectors_given,
        inline_adaptation_speed,
        memory_fading_factors,
        row(extra_coordinate_factors),
    )
    return pl.pallas_call(
        exchange,
        out_shape=jax.ShapeDtypeStruct((TOKENS, WIDTH), BF16),
        in_specs=[vmem] * 11,
        out_specs=vmem,
        scratch_shapes=SCRATCH,
        compiler_params=pltpu.CompilerParams(
            collective_id=0, has_side_effects=True, vmem_limit_bytes=56 << 20
        ),
        name="exchange",
    )(
        activation_entries,
        content_mapping_matrix,
        row(content_lagged_blend),
        *prepared,
        result_filter_given,
        row(group_layernorm_scaling),
        row(group_layernorm_offset),
    )


def solution(mesh):
    return jax.shard_map(
        shards,
        mesh=mesh,
        in_specs=(
            P("seq", "fsdp"),
            P("seq", "fsdp"),
            P("fsdp"),
            P("seq", "fsdp"),
            P("seq", "fsdp"),
            P("seq", "fsdp"),
            P("seq", "fsdp"),
            P("seq", "fsdp"),
            P("fsdp"),
            P("fsdp"),
            P("fsdp"),
        ),
        out_specs=P("seq", "fsdp"),
        check_vma=False,
    )
```

time: 373 us -> 70.5 us (0.19); the launches traced: 368 us -> 70.3 us
  other arithmetic: 109 us -> 0 us
  waiting for transfers between devices: 109 us -> 0 us
  local copies, waits for them, and re-layouts: 81 us -> 1.57 us
  Pallas kernels: 0 us -> 68.8 us
  matrix products: 48.5 us -> 0 us
  between operations: 13.7 us -> 0.01 us
  starting transfers between devices: 3.75 us -> 0 us
    all_gather x3 -> x0, waiting for transfers between devices: 108 us -> none  [the longest x1 95.9 us: prefix_2(): pieces = lax.all_gather(value, axis)]
    another operation x5 -> x0, other arithmetic: 103 us -> none  [the longest x4 79.3 us: block_step(): lax.linalg.triangular_solve(system_b, rhs, left_side=True, lower=True, un...]
    pallas_call x0 -> x2, Pallas kernels: none -> 68.8 us  [the longest x1 61.4 us: shards(): pl.pallas_call(exchange, out_shape=jax.ShapeDtypeStruct((TOKENS, WIDTH),...]
    squeeze x64 -> x0, local copies, waits for them, and re-layouts: 62.7 us -> none  [the longest x63 61.5 us: step(): longer = join(so_far, pieces[position])]
    dot_general x77 -> x0, matrix products: 45.9 us -> none  [the longest x63 28.1 us: combine_pairs(): jnp.einsum('hij,hjr->hir', later[:, :, GROUP_DIMENSION:], earlier, precis...]
    unnamed x31 -> x1, local copies, waits for them, and re-layouts: 5.74 us -> 1.57 us
  transfers between devices with their start and end apart: 4 -> 0, of which waited for: 2 -> 0; matrix products, arithmetic and copies ran while one was open for 35% -> 0% of each run, Pallas kernels for 0% -> 0%
where the time goes in v1:
time: 70.5 us; the launch traced here: 70.3 us
  Pallas kernels  68.8 us (98%)
  local copies, waits for them, and re-layouts  1.57 us (2%)
    pallas_call x1, Pallas kernels, shards(): pl.pallas_call(exchange, out_shape=jax.ShapeDtypeStruct((TOKENS, WIDTH),...  61.4 us
    pallas_call x1, Pallas kernels, shards(): pl.pallas_call(prepare, out_shape=[jax.ShapeDtypeStruct(shape, kind) for...  7.39 us
    unnamed x1, local copies, waits for them, and re-layouts  1.57 us

profile of v1, /device:TPU:57, one launch (start us, length us, event | category | flops | bytes accessed | tf_op | source)
XLA Modules:
  0.0 70.3 jit_solution(6361017107597657396)
XLA Ops:
  0.0 7.4 %prepare.1 = (bf16[8,128,256]{2,1,0:T(8,128)(2,1)}, bf16[8,128,128]{2,1,0:T(8,128)(2,1)}, bf16[8,64,256]{2,1,0:T(8,128)(2,1)}, bf16[8,64,128]{2,1,0:T(8,128)(2,1)}, f32[128,512]{1,0:T(8,128)}) custom-call(bf16[128,512]{1,0:T(8,128)(2,1)} %r_ref.1, bf16[128,512]{1,0:T(8,128)(2,1)} %k_ref.1, bf16[128,512]{1,0:T(8,128)(2,1)} %a_ref.1, f32[128,512]{1,0:T(8,128)} %w_ref.2, ...), custom_call_target="tpu_custom_call" | custom-call | tf_op jit(solution)/shard_map/prepare/pallas_call | solution.py:525
  7.4 61.4 %exchange.1 = bf16[128,512]{1,0:T(8,128)(2,1)} custom-call(bf16[128,512]{1,0:T(8,128)(2,1)} %x_ref.1, bf16[64,512]{1,0:T(8,128)(2,1)} %w_ref.3, f32[1,512]{1,0:T(1,128)} %bitcast.5, bf16[8,128,256]{2,1,0:T(8,128)(2,1)} %get-tuple-element.10.y_ref, bf16[8,128,128]{2,1,0:T(8,128)(2,1)} %get-tuple-element.11.q_ref, ...), custom_call_target="tpu_custom_call" | custom-call | tf_op jit(solution)/shard_map/exchange/pallas_call | solution.py:539
  68.8 1.6 %copy.13 = bf16[128,512]{1,0:T(8,128)(2,1)} copy(bf16[128,512]{1,0:T(8,128)(2,1)} %exchange.1) | data formatting | bytes 262144

commit v2 on v1

--- a/solution.py
+++ b/solution.py
@@ -72,6 +72,7 @@
     cumul = w_ref[...]
     for level in range(7):
         cumul = cumul * shift_rows(cumul, 1 << level, 1.0)
+    yield
     before = shift_rows(cumul, 1, 1.0)
     inverse = 1.0 / cumul
     end = cumul[TOKENS - 1 :, :]
@@ -97,25 +98,28 @@
         left = wide_left(
             cat(erase_h[:, at], rec_h[:, at], axis=0), cat(erase_l[:, at], rec_l[:, at], axis=0)
         )
-        right = wide_left(
-            cat(write_h[:, at], key_h[:, at], axis=0), cat(write_l[:, at], key_l[:, at], axis=0)
-        )
-        right = cat(right[:, :HEAD], right[:, :HEAD], right[:, HEAD : 2 * HEAD], axis=1)
-        grams.append(dot_nt(left, right))
+        high = cat(write_h[:, at], key_h[:, at], axis=0)
+        low = cat(write_l[:, at], key_l[:, at], axis=0)
+        grams.append(dot_nt(left, cat(high, high, low, axis=1)))
+        if h == HEADS // 2 - 1:
+            yield
     systems = [jnp.where(strict, gram[:TOKENS, :TOKENS], 0.0) for gram in grams]
     halves = [split(system) for system in systems]
     for h in range(HEADS):
         solves.append(eye + jnp.where(differ == 1, systems[h], 0.0))
+    yield
     for level in range(1, 7):
         mask = (differ >> level) == 1
         for h in range(HEADS):
             rough = solves[h].astype(BF16)
             part = jnp.where(mask, halves[h][0], jnp.zeros_like(halves[h][0]))
             solves[h] = solves[h] + dot(rough, dot(part, rough).astype(BF16))
+        yield
     for h in range(HEADS):
         high, low = split(solves[h])
         left_over = eye - solves[h] + dot(wide_left(*halves[h]), wide_right(high, low))
         solves[h] = solves[h] + dot(high, left_over.astype(BF16))
+    yield
     for pair in range(HEADS // 2):
         wide = slice(2 * HEAD * pair, 2 * HEAD * (pair + 1))
         write_t = write_end[:, wide].T
@@ -144,15 +148,7 @@
             h_ref[h] = cat(*split(key_t[mine] + out[TOKENS:, :TOKENS]), axis=1)
             diagonal = jnp.where(small_eye, end[:, at], 0.0)
             g_ref[h] = cat(*split(diagonal + out[TOKENS:, TOKENS:]), axis=1)
-
-
-PREPARED = (
-    ((HEADS, TOKENS, 2 * TOKENS), BF16),
-    ((HEADS, TOKENS, 2 * HEAD), BF16),
-    ((HEADS, HEAD, 2 * TOKENS), BF16),
-    ((HEADS, HEAD, 2 * HEAD), BF16),
-    ((TOKENS, WIDTH), F32),
-)
+        yield
 
 
 def chain_step(g, z):
@@ -168,9 +164,11 @@
     return cat(*split(x), axis=1)
 
 
-def exchange(
-    x_ref, w_ref, blend_ref, y_ref, q_ref, h_ref, g_ref, coef_ref, gate_ref, scale_ref, offset_ref,
+def time_mix(
+    x_hbm, w_ref, r_hbm, k_hbm, a_hbm, decay_hbm, gate_hbm, blend_ref, bonus_ref, scale_ref, offset_ref,
     out_ref,
+    x_ref, r_ref, k_ref, a_ref, decay_ref, gate_ref,
+    y_ref, q_ref, h_ref, g_ref, coef_ref,
     prev_buf, x_send, xg, wa, wb, p_send, p_recv,
     g_row, g_col, z_chain, z_all, z_row,
     l_send, l_row, t_send, t_col, s_send, s_in,
@@ -204,10 +202,32 @@
             entry[1] = True
             entry[0].wait_recv()
 
-    own_a = pltpu.make_async_copy(w_ref.at[:, pl.ds(0, 256)], wa.at[y, x], local.at[0])
-    own_b = pltpu.make_async_copy(w_ref.at[:, pl.ds(256, 256)], wb.at[y, x], local.at[1])
-    own_a.start()
-    own_b.start()
+    def finish():
+        for entry in waiting:
+            entry[0].wait_send()
+        for d, _, copy in conditional:
+
+            @pl.when(y + d < NY)
+            def _(copy=copy):
+                copy.wait_send()
+
+    loads = [
+        pltpu.make_async_copy(source, target, local.at[n])
+        for n, (source, target) in enumerate(
+            (
+                (w_ref.at[:, pl.ds(0, 256)], wa.at[y, x]),
+                (w_ref.at[:, pl.ds(256, 256)], wb.at[y, x]),
+                (x_hbm, x_ref),
+                (r_hbm, r_ref),
+                (k_hbm, k_ref),
+                (a_hbm, a_ref),
+                (decay_hbm, decay_ref),
+                (gate_hbm, gate_ref),
+            )
+        )
+    ]
+    for load in loads:
+        load.start()
     for d in range(NY):
         t_col[d] = jnp.zeros((HEAD, 2 * HEAD), BF16)
     barrier = pltpu.get_barrier_semaphore()
@@ -218,14 +238,14 @@
     for partner in partners:
         pl.semaphore_signal(barrier, inc=1, device_id=partner, device_id_type=MESH)
     pl.semaphore_wait(barrier, len(partners))
-    own_a.wait()
-    own_b.wait()
+    for load in loads:
+        load.wait()
 
     right, left = (x + 1) % NX, (x + NX - 1) % NX
     sides = (1, -1)
 
+    a_in = [copy_to(wa.at[y, x], wa.at[y, x], chip(y, (x + d) % NX)) for d in range(1, NX)]
     prev = copy_to(x_ref.at[pl.ds(TOKENS - 16, 16)], prev_buf, at_seq((s + 1) % count))
-    a_in = [copy_to(wa.at[y, x], wa.at[y, x], chip(y, (x + d) % NX)) for d in range(1, NX)]
 
     yb = {}
     xb = {}
@@ -256,8 +276,86 @@
             arrived(xb[-1, offset])
             copy_to(wb.at[row, right], wb.at[row, right], chip(y, left))
 
+    zx, ya = {}, {}
+
+    def send_zx(step, sub):
+        part = core if sub == 0 else 1 - core
+        for side in sides:
+            if step == NZ // 2 and side != sides[sub]:
+                continue
+            if step > 1:
+                arrived(zx[side, step - 1, sub])
+            block = (z + NZ - side * (step - 1)) % NZ
+            zx[side, step, sub] = copy_to(
+                xg.at[block, part], xg.at[block, part], {"fsdp": (z + NZ + side) % NZ}
+            )
+
+    def send_ya(step, sub):
+        for side in sides:
+            if step == NY // 2 and side != sides[sub]:
+                continue
+            if step > 1:
+                arrived(ya[side, step - 1, sub])
+            row = row_at(-side * (step - 1))
+            part = wa.at[row, pl.ds(2 * sub, 2)]
+            ya[side, step, sub] = copy_to(part, part, chip(row_at(side), x))
+
+    def row_chain():
+        for entry in g_in:
+            arrived(entry)
+        wide = z_chain.shape[1]
+        lane, line = iota((HEAD, wide), 1), iota((HEAD, wide), 0)
+        chain = (lane == line + ROW * HEAD).astype(F32)
+        for j in range(ROW):
+            z_all[j] = cat(*split(chain), axis=1)
+            chain = chain_step(g_row[j], chain) + (lane == line + j * HEAD).astype(F32)
+        z_chain[...] = chain
+
+    def send_g_col():
+        total = pack(z_chain[...][:, ROW * HEAD : (ROW + 1) * HEAD])
+        g_col[y] = total
+        for d in range(1, NY):
+            n = next(counter)
+            conditional.append(
+                (d, n, pltpu.make_async_remote_copy(
+                    src_ref=g_col.at[y], dst_ref=g_col.at[y], send_sem=send.at[n], recv_sem=recv.at[n],
+                    device_id=chip((y + d) % NY, x), device_id_type=MESH,
+                ))
+            )
+
+            @pl.when(y + d < NY)
+            def _(copy=conditional[-1][2]):
+                copy.start()
+
+    def column_chain():
+        for d, _, copy in conditional[: NY - 1]:
+
+            @pl.when(y >= d)
+            def _(copy=copy):
+                copy.wait_recv()
+
+        lane, line = iota((HEAD, NY * HEAD), 1), iota((HEAD, NY * HEAD), 0)
+        chain = jnp.zeros((HEAD, NY * HEAD), F32)
+        for q in range(NY - 1):
+            longer = chain_step(g_col[q], chain) + (lane == line + q * HEAD).astype(F32)
+            chain = jnp.where(q < y, longer, chain)
+        z_row[...] = cat(*split(chain), axis=0)
+
+    stages = prepare(
+        r_ref, k_ref, a_ref, decay_ref, bonus_ref, y_ref, q_ref, h_ref, g_ref, coef_ref
+    )
+
+    def compute(steps=1):
+        for _ in range(steps):
+            next(stages, None)
+
     send_yb(1)
     send_xb(0)
+    compute()
+    for entry in a_in:
+        arrived(entry)
+    send_ya(1, 0)
+    send_ya(1, 1)
 
     arrived(prev)
     own = x_ref[...].astype(F32)
@@ -272,111 +370,55 @@
     mate = at_seq(s + 1 - 2 * core)
     mate_x = copy_to(x_send, xg.at[z, core], mate)
 
-    zx, ya = {}, {}
-
-    def send_zx(step, sub):
-        part = core if sub == 0 else 1 - core
-        for side in sides:
-            if step == NZ // 2 and side != sides[sub]:
-                continue
-            if step > 1:
-                arrived(zx[side, step - 1, sub])
-            block = (z + NZ - side * (step - 1)) % NZ
-            zx[side, step, sub] = copy_to(
-                xg.at[block, part], xg.at[block, part], {"fsdp": (z + NZ + side) % NZ}
-            )
-
-    def send_ya(step, sub):
-        for side in sides:
-            if step == NY // 2 and side != sides[sub]:
-                continue
-            if step > 1:
-                arrived(ya[side, step - 1, sub])
-            row = row_at(-side * (step - 1))
-            part = wa.at[row, pl.ds(2 * sub, 2)]
-            ya[side, step, sub] = copy_to(part, part, chip(row_at(side), x))
-
     send_zx(1, 0)
-    for entry in a_in:
-        arrived(entry)
-    send_ya(1, 0)
-    send_ya(1, 1)
+    send_yb(2)
+    send_xb(-1)
+    send_xb(1)
+    forward_xb(0)
     arrived(mate_x)
     send_zx(1, 1)
+    compute()
+    send_ya(2, 0)
+    send_zx(2, 0)
+    send_yb(3)
+    send_xb(-2)
+    send_xb(2)
+    forward_xb(-1)
+    forward_xb(1)
+    compute(2)
+    send_ya(2, 1)
+    send_zx(2, 1)
+    send_yb(4)
+    send_xb(-3)
+    send_xb(3)
+    forward_xb(-2)
+    forward_xb(2)
+    compute(2)
+    send_ya(3, 0)
+    send_zx(3, 0)
+    arrived(yb[1, NY // 2])
+    send_xb(-4)
+    forward_xb(-3)
+    forward_xb(3)
+    compute(2)
+    send_ya(3, 1)
+    send_zx(3, 1)
+    forward_xb(-4)
+    compute(3)
+    send_ya(4, 0)
+    send_zx(4, 0)
+    compute(2)
+    send_ya(4, 1)
+    send_zx(4, 1)
+    compute(100)
 
     g_in = []
     g_row[place] = g_ref[place]
     for d in range(1, ROW):
         to = (place + d) % ROW
         g_in.append(copy_to(g_ref.at[to], g_row.at[place], at_seq(y * ROW + to)))
-
-    def round_of(step):
-        for sub in range(2):
-            send_ya(step, sub)
-            send_zx(step, sub)
-            if sub == 0:
-                send_yb(step)
-                for offset in (-(step - 1), step - 1):
-                    send_xb(offset)
-            else:
-                if step == 2:
-                    forward_xb(0)
-                else:
-                    for offset in (-(step - 2), step - 2):
-                        forward_xb(offset)
-
-    def row_chain():
-        for entry in g_in:
-            arrived(entry)
-        wide = z_chain.shape[1]
-        lane, line = iota((HEAD, wide), 1), iota((HEAD, wide), 0)
-        chain = (lane == line + ROW * HEAD).astype(F32)
-        for j in range(ROW):
-            z_all[j] = cat(*split(chain), axis=1)
-            chain = chain_step(g_row[j], chain) + (lane == line + j * HEAD).astype(F32)
-        z_chain[...] = chain
-
-    def send_g_col():
-        total = pack(z_chain[...][:, ROW * HEAD : (ROW + 1) * HEAD])
-        g_col[y] = total
-        for d in range(1, NY):
-            n = next(counter)
-            conditional.append(
-                (d, n, pltpu.make_async_remote_copy(
-                    src_ref=g_col.at[y], dst_ref=g_col.at[y], send_sem=send.at[n], recv_sem=recv.at[n],
-                    device_id=chip((y + d) % NY, x), device_id_type=MESH,
-                ))
-            )
-
-            @pl.when(y + d < NY)
-            def _(copy=conditional[-1][2]):
-                copy.start()
-
-    def column_chain():
-        for d, _, copy in conditional[: NY - 1]:
-
-            @pl.when(y >= d)
-            def _(copy=copy):
-                copy.wait_recv()
-
-        lane, line = iota((HEAD, NY * HEAD), 1), iota((HEAD, NY * HEAD), 0)
-        chain = jnp.zeros((HEAD, NY * HEAD), F32)
-        for q in range(NY - 1):
-            longer = chain_step(g_col[q], chain) + (lane == line + q * HEAD).astype(F32)
-            chain = jnp.where(q < y, longer, chain)
-        z_row[...] = cat(*split(chain), axis=0)
-
-    round_of(2)
     row_chain()
-    round_of(3)
     send_g_col()
-    round_of(4)
-    column_chain()
-    arrived(yb[1, NY // 2])
-    send_xb(-4)
-    forward_xb(-3)
-    forward_xb(3)
-    forward_xb(-4)
     for entry in waiting:
         arrived(entry)
 
@@ -408,6 +450,7 @@
         to = (place + d) % ROW
         l_in.append(copy_to(l_send.at[to], l_row.at[place], at_seq(y * ROW + to)))
     l_row[place] = l_send[place]
+    column_chain()
     chain = z_chain[...][:, : ROW * HEAD]
     row_total = cat(*split(chain), axis=0)
     for entry in l_in:
@@ -469,17 +512,22 @@
     normed = centre * lax.rsqrt(spread + NORM_EPS) * scale_ref[...] + offset_ref[...]
     out_ref[...] = ((normed + extra) * gate).astype(BF16)
 
-    for entry in waiting:
-        entry[0].wait_send()
-    for d, _, copy in conditional:
-
-        @pl.when(y + d < NY)
-        def _(copy=copy):
-            copy.wait_send()
+    finish()
 
 
 COPIES = 128
 SCRATCH = (
+    pltpu.VMEM((TOKENS, WIDTH), BF16),
+    pltpu.VMEM((TOKENS, WIDTH), BF16),
+    pltpu.VMEM((TOKENS, WIDTH), BF16),
+    pltpu.VMEM((TOKENS, WIDTH), BF16),
+    pltpu.VMEM((TOKENS, WIDTH), F32),
+    pltpu.VMEM((TOKENS, WIDTH), BF16),
+    pltpu.VMEM((HEADS, TOKENS, 2 * TOKENS), BF16),
+    pltpu.VMEM((HEADS, TOKENS, 2 * HEAD), BF16),
+    pltpu.VMEM((HEADS, HEAD, 2 * TOKENS), BF16),
+    pltpu.VMEM((HEADS, HEAD, 2 * HEAD), BF16),
+    pltpu.VMEM((TOKENS, WIDTH), F32),
     pltpu.VMEM((16, WIDTH), BF16),
     pltpu.VMEM((TOKENS, 256), BF16),
     pltpu.VMEM((NZ, 2, TOKENS, 256), BF16),
@@ -500,7 +548,7 @@
     pltpu.VMEM((HEADS, HEAD, 2 * HEAD), BF16),
     pltpu.SemaphoreType.DMA((COPIES,)),
     pltpu.SemaphoreType.DMA((COPIES,)),
-    pltpu.SemaphoreType.DMA((2,)),
+    pltpu.SemaphoreType.DMA((8,)),
 )
 
 
@@ -522,36 +570,27 @@
     def row(vector):
         return vector.reshape(1, WIDTH)
 
-    prepared = pl.pallas_call(
-        prepare,
-        out_shape=[jax.ShapeDtypeStruct(shape, kind) for shape, kind in PREPARED],
-        in_specs=[vmem] * 5,
-        out_specs=[vmem] * len(PREPARED),
-        compiler_params=pltpu.CompilerParams(vmem_limit_bytes=56 << 20),
-        name="prepare",
-    )(
-        acceptance_vectors,
-        address_vectors_given,
-        inline_adaptation_speed,
-        memory_fading_factors,
-        row(extra_coordinate_factors),
-    )
+    hbm = pl.BlockSpec(memory_space=pl.ANY)
     return pl.pallas_call(
-        exchange,
+        time_mix,
         out_shape=jax.ShapeDtypeStruct((TOKENS, WIDTH), BF16),
-        in_specs=[vmem] * 11,
+        in_specs=[hbm] * 7 + [vmem] * 4,
         out_specs=vmem,
         scratch_shapes=SCRATCH,
         compiler_params=pltpu.CompilerParams(
             collective_id=0, has_side_effects=True, vmem_limit_bytes=56 << 20
         ),
-        name="exchange",
+        name="time_mix",
     )(
         activation_entries,
         content_mapping_matrix,
+        acceptance_vectors,
+        address_vectors_given,
+        inline_adaptation_speed,
+        memory_fading_factors,
+        result_filter_given,
         row(content_lagged_blend),
-        *prepared,
-        result_filter_given,
+        row(extra_coordinate_factors),
         row(group_layernorm_scaling),
         row(group_layernorm_offset),
     )

time: 70.5 us -> 63.4 us (0.90); the launches traced: 70.3 us -> 62.2 us
  Pallas kernels: 68.8 us -> 60.7 us
    pallas_call x2 -> x1, Pallas kernels: 68.8 us -> 60.7 us  [shards(): pl.pallas_call(time_mix, out_shape=jax.ShapeDtypeStruct((TOKENS, WIDTH),...]
where the time goes in v2:
time: 63.4 us; the launch traced here: 62.2 us
  Pallas kernels  60.7 us (96%)
  local copies, waits for them, and re-layouts  1.57 us (2%)
    pallas_call x1, Pallas kernels, shards(): pl.pallas_call(time_mix, out_shape=jax.ShapeDtypeStruct((TOKENS, WIDTH),...  60.7 us
    unnamed x1, local copies, waits for them, and re-layouts  1.57 us

profile of v2, /device:TPU:57, one launch (start us, length us, event | category | flops | bytes accessed | tf_op | source)
XLA Modules:
  0.0 62.2 jit_solution(2161373972434875312)
XLA Ops:
  0.0 60.7 %time_mix.1 = bf16[128,512]{1,0:T(8,128)(2,1)} custom-call(bf16[128,512]{1,0:T(8,128)(2,1)} %x_hbm.1, bf16[64,512]{1,0:T(8,128)(2,1)} %w_ref.1, bf16[128,512]{1,0:T(8,128)(2,1)} %r_hbm.1, bf16[128,512]{1,0:T(8,128)(2,1)} %k_hbm.1, bf16[128,512]{1,0:T(8,128)(2,1)} %a_hbm.1, f32[128,512]{1,0:T(8,128)} %decay_hbm.1, bf16[128,512]{1,0:T(8,128)(2,1)} %gate_hbm.1, ...), custom_call_target="tpu_custom_call" | custom-call | tf_op jit(solution)/shard_map/time_mix/pallas_call | solution.py:574
  60.7 1.6 %copy.13 = bf16[128,512]{1,0:T(8,128)(2,1)} copy(bf16[128,512]{1,0:T(8,128)(2,1)} %time_mix.1) | data formatting | bytes 262144

commit v3 on v2

--- a/solution.py
+++ b/solution.py
@@ -16,6 +16,9 @@
 WIDTH = HEAD * HEADS
 NX, NY, NZ = 4, 8, 8
 ROW = 2 * NX
+OFFSETS = (0, -1, 1, -2, 2, -3, 3, 4)
+SLOT = {offset: n for n, offset in enumerate(OFFSETS)} | {-4: 7}
+FAR_FIRST = (4, 3, 5, 2, 6, 1, 7)
 NORM_EPS = 0.00064
 UNIT_EPS = 1e-05
 
@@ -120,35 +123,39 @@
         left_over = eye - solves[h] + dot(wide_left(*halves[h]), wide_right(high, low))
         solves[h] = solves[h] + dot(high, left_over.astype(BF16))
     yield
+    inverses = [wide_left(*split(solve)) for solve in solves]
+    mixes = []
     for pair in range(HEADS // 2):
         wide = slice(2 * HEAD * pair, 2 * HEAD * (pair + 1))
         write_t = write_end[:, wide].T
+        for half in range(2):
+            h = 2 * pair + half
+            at = slice(HEAD * h, HEAD * (h + 1))
+            keyed = dot(inverses[h], wide_right(erase_h[:, at], erase_l[:, at]))
+            read_write = jnp.where(inclusive, grams[h][TOKENS:, :TOKENS], 0.0)
+            mine = slice(HEAD * half, HEAD * (half + 1))
+            mixes.append(wide_left(*split(cat(read_write, write_t[mine], axis=0))))
+            out = dot(mixes[h], wide_right(*split(keyed)))
+            q_ref[h] = cat(*split(rec[:, at] + out[:TOKENS]), axis=1)
+            diagonal = jnp.where(small_eye, end[:, at], 0.0)
+            g_ref[h] = cat(*split(diagonal + out[TOKENS:]), axis=1)
+        if pair % 2:
+            yield
+    for pair in range(HEADS // 2):
+        wide = slice(2 * HEAD * pair, 2 * HEAD * (pair + 1))
         key_t = key_end[:, wide].T
         for half in range(2):
             h = 2 * pair + half
-            at = slice(HEAD * h, HEAD * (h + 1))
             gram = grams[h]
-            erase_key = split(jnp.where(strict, gram[:TOKENS, TOKENS:], 0.0))
-            read_write = jnp.where(inclusive, gram[TOKENS:, :TOKENS], 0.0)
+            erase_key = jnp.where(strict, gram[:TOKENS, TOKENS:], 0.0)
             read_key = jnp.where(inclusive, gram[TOKENS:, TOKENS:], 0.0)
-            both = dot(
-                wide_left(*split(solves[h])),
-                wide_right(
-                    cat(erase_key[0], erase_h[:, at], axis=1),
-                    cat(erase_key[1], erase_l[:, at], axis=1),
-                ),
-            )
+            valued = dot(inverses[h], wide_right(*split(erase_key)))
+            out = dot(mixes[h], wide_right(*split(valued)))
             mine = slice(HEAD * half, HEAD * (half + 1))
-            out = dot(
-                wide_left(*split(cat(read_write, write_t[mine], axis=0))),
-                wide_right(*split(both)),
-            )
-            y_ref[h] = cat(*split(read_key + out[:TOKENS, :TOKENS]), axis=1)
-            q_ref[h] = cat(*split(rec[:, at] + out[:TOKENS, TOKENS:]), axis=1)
-            h_ref[h] = cat(*split(key_t[mine] + out[TOKENS:, :TOKENS]), axis=1)
-            diagonal = jnp.where(small_eye, end[:, at], 0.0)
-            g_ref[h] = cat(*split(diagonal + out[TOKENS:, TOKENS:]), axis=1)
-        yield
+            y_ref[h] = cat(*split(read_key + out[:TOKENS]), axis=1)
+            h_ref[h] = cat(*split(key_t[mine] + out[TOKENS:]), axis=1)
+        if pair % 2:
+            yield
 
 
 def chain_step(g, z):
@@ -202,6 +209,15 @@
             entry[1] = True
             entry[0].wait_recv()
 
+    def arrived_from_below(number=None):
+        for entry in conditional[:number]:
+            if not entry[1]:
+                entry[1] = True
+
+                @pl.when(y >= entry[0])
+                def _(copy=entry[2]):
+                    copy.wait_recv()
+
     def finish():
         for entry in waiting:
             entry[0].wait_send()
@@ -211,13 +227,23 @@
             def _(copy=copy):
                 copy.wait_send()
 
+    mate = at_seq(s + 1 - 2 * core)
+    sides = (1, -1)
+    barrier = pltpu.get_barrier_semaphore()
+    partners = [chip(y, (x + d) % NX) for d in range(1, NX)]
+    partners += [chip((y + NY + side) % NY, x) for side in sides]
+    partners += [{"fsdp": (z + NZ + side) % NZ} for side in sides]
+    partners += [mate, at_seq((s + count - 1 + 2 * core) % count)]
+    for partner in partners:
+        pl.semaphore_signal(barrier, inc=1, device_id=partner, device_id_type=MESH)
+    own_a, own_b = w_ref.at[:, pl.ds(0, 256)], w_ref.at[:, pl.ds(256, 256)]
     loads = [
         pltpu.make_async_copy(source, target, local.at[n])
         for n, (source, target) in enumerate(
             (
-                (w_ref.at[:, pl.ds(0, 256)], wa.at[y, x]),
-                (w_ref.at[:, pl.ds(256, 256)], wb.at[y, x]),
                 (x_hbm, x_ref),
+                (own_a, wa.at[0, x]),
+                (own_b, wb.at[0, x]),
                 (r_hbm, r_ref),
                 (k_hbm, k_ref),
                 (a_hbm, a_ref),
@@ -230,75 +256,56 @@
         load.start()
     for d in range(NY):
         t_col[d] = jnp.zeros((HEAD, 2 * HEAD), BF16)
-    barrier = pltpu.get_barrier_semaphore()
-    partners = [at_seq(y * ROW + (place + d) % ROW) for d in range(1, ROW)]
-    partners += [chip((y + d) % NY, x) for d in range(1, NY)]
-    partners += [{"fsdp": (z + 1) % NZ}, {"fsdp": (z + NZ - 1) % NZ}]
-    partners += [at_seq((s + 1) % count), at_seq((s + count - 1) % count)]
-    for partner in partners:
-        pl.semaphore_signal(barrier, inc=1, device_id=partner, device_id_type=MESH)
     pl.semaphore_wait(barrier, len(partners))
-    for load in loads:
-        load.wait()
-
-    right, left = (x + 1) % NX, (x + NX - 1) % NX
-    sides = (1, -1)
-
-    a_in = [copy_to(wa.at[y, x], wa.at[y, x], chip(y, (x + d) % NX)) for d in range(1, NX)]
-    prev = copy_to(x_ref.at[pl.ds(TOKENS - 16, 16)], prev_buf, at_seq((s + 1) % count))
-
-    yb = {}
-    xb = {}
+
+    yb, ya, zx = {}, {}, {}
 
     def row_at(offset):
         return (y + offset + NY) % NY
 
     def send_yb(step):
+        if step > 1:
+            for side in sides:
+                arrived(yb[side, step - 1])
         for side in sides:
-            if step > 1:
-                arrived(yb[side, step - 1])
-            if step == NY // 2 and side < 0:
-                continue
-            row = row_at(-side * (step - 1))
-            yb[side, step] = copy_to(wb.at[row, x], wb.at[row, x], chip(row_at(side), x))
-
-    def send_xb(offset):
-        row = row_at(offset)
-        for side, to in ((1, right), (-1, left)):
-            xb[side, offset] = copy_to(wb.at[row, x], wb.at[row, x], chip(y, to))
-
-    def forward_xb(offset):
-        row = row_at(offset)
-        if offset % 2 == 0:
-            arrived(xb[1, offset])
-            copy_to(wb.at[row, left], wb.at[row, left], chip(y, right))
-        else:
-            arrived(xb[-1, offset])
-            copy_to(wb.at[row, right], wb.at[row, right], chip(y, left))
-
-    zx, ya = {}, {}
+            source = own_b if step == 1 else wb.at[SLOT[-side * (step - 1)], x]
+            yb[side, step] = copy_to(source, wb.at[SLOT[-side * step], x], chip(row_at(side), x))
+            if step == 3 and side > 0:
+                yb[side, 4] = copy_to(
+                    wb.at[SLOT[-2 * side], x], wb.at[SLOT[4], x], chip(row_at(2 * side), x)
+                )
+
+    def send_xb(first, number):
+        part = wb.at[pl.ds(first, number), x]
+        for d in (2, 1, 3):
+            copy_to(part, part, chip(y, (x + d) % NX))
 
     def send_zx(step, sub):
         part = core if sub == 0 else 1 - core
+        if step > 1:
+            for side in sides:
+                arrived(zx[side, step - 1, sub])
         for side in sides:
-            if step == NZ // 2 and side != sides[sub]:
-                continue
-            if step > 1:
-                arrived(zx[side, step - 1, sub])
             block = (z + NZ - side * (step - 1)) % NZ
-            zx[side, step, sub] = copy_to(
-                xg.at[block, part], xg.at[block, part], {"fsdp": (z + NZ + side) % NZ}
+            held = xg.at[block, part]
+            if step == 3 and side == sides[sub]:
+                zx[side, 4, sub] = copy_to(held, held, {"fsdp": (z + NZ + 2 * side) % NZ})
+            zx[side, step, sub] = copy_to(held, held, {"fsdp": (z + NZ + side) % NZ})
+
+    def send_ya(step, sub):
+        if step > 1:
+            for side in sides:
+                arrived(ya[side, step - 1, sub])
+        pair = pl.ds(2 * sub, 2)
+        for side in sides:
+            source = wa.at[SLOT[-side * (step - 1)], pair]
+            if step == 3 and side == sides[sub]:
+                ya[side, 4, sub] = copy_to(
+                    source, wa.at[SLOT[4], pair], chip(row_at(2 * side), x)
+                )
+            ya[side, step, sub] = copy_to(
+                source, wa.at[SLOT[-side * step], pair], chip(row_at(side), x)
             )
-
-    def send_ya(step, sub):
-        for side in sides:
-            if step == NY // 2 and side != sides[sub]:
-                continue
-            if step > 1:
-                arrived(ya[side, step - 1, sub])
-            row = row_at(-side * (step - 1))
-            part = wa.at[row, pl.ds(2 * sub, 2)]
-            ya[side, step, sub] = copy_to(part, part, chip(row_at(side), x))
 
     def row_chain():
         for entry in g_in:
@@ -314,13 +321,13 @@
     def send_g_col():
         total = pack(z_chain[...][:, ROW * HEAD : (ROW + 1) * HEAD])
         g_col[y] = total
-        for d in range(1, NY):
+        for d in FAR_FIRST:
             n = next(counter)
             conditional.append(
-                (d, n, pltpu.make_async_remote_copy(
+                [d, False, pltpu.make_async_remote_copy(
                     src_ref=g_col.at[y], dst_ref=g_col.at[y], send_sem=send.at[n], recv_sem=recv.at[n],
                     device_id=chip((y + d) % NY, x), device_id_type=MESH,
-                ))
+                )]
             )
 
             @pl.when(y + d < NY)
@@ -328,12 +335,7 @@
                 copy.start()
 
     def column_chain():
-        for d, _, copy in conditional[: NY - 1]:
-
-            @pl.when(y >= d)
-            def _(copy=copy):
-                copy.wait_recv()
-
+        arrived_from_below(NY - 1)
         lane, line = iota((HEAD, NY * HEAD), 1), iota((HEAD, NY * HEAD), 0)
         chain = jnp.zeros((HEAD, NY * HEAD), F32)
         for q in range(NY - 1):
@@ -349,13 +351,12 @@
         for _ in range(steps):
             next(stages, None)
 
+    a_in = [copy_to(own_a, wa.at[0, x], chip(y, (x + d) % NX)) for d in (2, 1, 3)]
+    prev = copy_to(x_hbm.at[pl.ds(TOKENS - 16, 16)], prev_buf, at_seq((s + 1) % count))
     send_yb(1)
-    send_xb(0)
+    for load in loads:
+        load.wait()
     compute()
-    for entry in a_in:
-        arrived(entry)
-    send_ya(1, 0)
-    send_ya(1, 1)
 
     arrived(prev)
     own = x_ref[...].astype(F32)
@@ -367,68 +368,49 @@
     is_even = core == 0
     xg[z, core] = jnp.where(is_even, even, odd)
     x_send[...] = jnp.where(is_even, odd, even)
-    mate = at_seq(s + 1 - 2 * core)
     mate_x = copy_to(x_send, xg.at[z, core], mate)
-
     send_zx(1, 0)
-    send_yb(2)
-    send_xb(-1)
-    send_xb(1)
-    forward_xb(0)
+    for entry in a_in:
+        arrived(entry)
+    send_ya(1, 0)
+    send_ya(1, 1)
     arrived(mate_x)
     send_zx(1, 1)
-    compute()
+    send_yb(2)
+    send_xb(0, 3)
+    compute(2)
+    send_zx(2, 0)
     send_ya(2, 0)
-    send_zx(2, 0)
+    send_zx(2, 1)
+    send_ya(2, 1)
     send_yb(3)
-    send_xb(-2)
-    send_xb(2)
-    forward_xb(-1)
-    forward_xb(1)
-    compute(2)
-    send_ya(2, 1)
-    send_zx(2, 1)
-    send_yb(4)
-    send_xb(-3)
-    send_xb(3)
-    forward_xb(-2)
-    forward_xb(2)
-    compute(2)
+    send_xb(3, 2)
+    compute(3)
+    send_zx(3, 0)
     send_ya(3, 0)
-    send_zx(3, 0)
-    arrived(yb[1, NY // 2])
-    send_xb(-4)
-    forward_xb(-3)
-    forward_xb(3)
-    compute(2)
+    send_zx(3, 1)
     send_ya(3, 1)
-    send_zx(3, 1)
-    forward_xb(-4)
-    compute(3)
-    send_ya(4, 0)
-    send_zx(4, 0)
-    compute(2)
-    send_ya(4, 1)
-    send_zx(4, 1)
-    compute(100)
+    for side, step in ((1, 3), (-1, 3), (1, 4)):
+        arrived(yb[side, step])
+    send_xb(5, 3)
+    compute(6)
 
     g_in = []
-    g_row[place] = g_ref[place]
-    for d in range(1, ROW):
+    for d in FAR_FIRST:
         to = (place + d) % ROW
         g_in.append(copy_to(g_ref.at[to], g_row.at[place], at_seq(y * ROW + to)))
-    row_chain()
-    send_g_col()
+    g_row[place] = g_ref[place]
+    compute(100)
     for entry in waiting:
-        arrived(entry)
-
+        if not any(entry is other for other in g_in):
+            arrived(entry)
     parts = {}
     for mine in (False, True):
         block = core if mine else 1 - core
         for half, weights in enumerate((wa, wb)):
             total = jnp.zeros((TOKENS, 256), F32)
-            for row in range(NY):
-                total = total + dot(xg[row, block], weights[row].reshape(256, 256))
+            for slot, offset in enumerate(OFFSETS):
+                total = total + dot(xg[row_at(offset), block], weights[slot].reshape(256, 256))
             if mine:
                 parts[half] = total
             else:
@@ -446,11 +428,12 @@
         doubled.append(cat(v, v, axis=0))
         l_send[h] = pack(dot(h_ref[h], doubled[h]))
     l_in = []
-    for d in range(1, ROW):
+    for d in FAR_FIRST:
         to = (place + d) % ROW
         l_in.append(copy_to(l_send.at[to], l_row.at[place], at_seq(y * ROW + to)))
     l_row[place] = l_send[place]
-    column_chain()
+    row_chain()
+    send_g_col()
     chain = z_chain[...][:, : ROW * HEAD]
     row_total = cat(*split(chain), axis=0)
     for entry in l_in:
@@ -458,14 +441,13 @@
     lows = l_row[...].reshape(ROW * HEAD, 2 * HEAD)
     total = fold(dot(row_total, lows))
     t_send[...] = pack(total[:HEAD] + total[HEAD:])
-    first = len(conditional)
-    for d in range(1, NY):
+    for d in FAR_FIRST:
         n = next(counter)
         conditional.append(
-            (d, n, pltpu.make_async_remote_copy(
+            [d, False, pltpu.make_async_remote_copy(
                 src_ref=t_send, dst_ref=t_col.at[y], send_sem=send.at[n], recv_sem=recv.at[n],
                 device_id=chip((y + d) % NY, x), device_id_type=MESH,
-            ))
+            )]
         )
 
         @pl.when(y + d < NY)
@@ -482,12 +464,8 @@
     extra = coef_ref[...] * value.astype(F32)
     gate = gate_ref[...].astype(F32)
 
-    for d, _, copy in conditional[first:]:
-
-        @pl.when(y >= d)
-        def _(copy=copy):
-            copy.wait_recv()
-
+    column_chain()
+    arrived_from_below()
     entering = fold(dot(z_row[...], t_col[...].reshape(NY * HEAD, 2 * HEAD)))
     entering = pack(entering[:HEAD] + entering[HEAD:])
     twice = cat(entering, entering, axis=0)
@@ -497,7 +475,7 @@
         )
         s_send[j] = pack(fold(from_row[j] + dot(both, twice)))
     s_wait = []
-    for d in range(1, ROW):
+    for d in FAR_FIRST:
         to = (place + d) % ROW
         s_wait.append(copy_to(s_send.at[to], s_in.at[place], at_seq(y * ROW + to)))
     s_in[place] = s_send[place]

time: 63.4 us -> 58.5 us (0.923); the launches traced: 62.2 us -> 58.4 us
  Pallas kernels: 60.7 us -> 56.8 us
    pallas_call x1, Pallas kernels: 60.7 us -> 56.8 us  [shards(): pl.pallas_call(time_mix, out_shape=jax.ShapeDtypeStruct((TOKENS, WIDTH),...]
where the time goes in v3:
time: 58.5 us; the launch traced here: 58.4 us
  Pallas kernels  56.8 us (97%)
  local copies, waits for them, and re-layouts  1.57 us (3%)
    pallas_call x1, Pallas kernels, shards(): pl.pallas_call(time_mix, out_shape=jax.ShapeDtypeStruct((TOKENS, WIDTH),...  56.8 us
    unnamed x1, local copies, waits for them, and re-layouts  1.57 us

profile of v3, /device:TPU:57, one launch (start us, length us, event | category | flops | bytes accessed | tf_op | source)
XLA Modules:
  0.0 58.4 jit_solution(12341979314891759212)
XLA Ops:
  0.0 56.8 %time_mix.1 = bf16[128,512]{1,0:T(8,128)(2,1)} custom-call(bf16[128,512]{1,0:T(8,128)(2,1)} %x_hbm.1, bf16[64,512]{1,0:T(8,128)(2,1)} %w_ref.1, bf16[128,512]{1,0:T(8,128)(2,1)} %r_hbm.1, bf16[128,512]{1,0:T(8,128)(2,1)} %k_hbm.1, bf16[128,512]{1,0:T(8,128)(2,1)} %a_hbm.1, f32[128,512]{1,0:T(8,128)} %decay_hbm.1, bf16[128,512]{1,0:T(8,128)(2,1)} %gate_hbm.1, ...), custom_call_target="tpu_custom_call" | custom-call | tf_op jit(solution)/shard_map/time_mix/pallas_call | solution.py:552
  56.8 1.6 %copy.13 = bf16[128,512]{1,0:T(8,128)(2,1)} copy(bf16[128,512]{1,0:T(8,128)(2,1)} %time_mix.1) | data formatting | bytes 262144

commit v4 on v3

--- a/solution.py
+++ b/solution.py
@@ -278,7 +278,10 @@
     def send_xb(first, number):
         part = wb.at[pl.ds(first, number), x]
         for d in (2, 1, 3):
-            copy_to(part, part, chip(y, (x + d) % NX))
+            if first == 0:
+                copy_to(own_b, wb.at[0, x], chip(y, (x + d) % NX))
+            else:
+                copy_to(part, part, chip(y, (x + d) % NX))
 
     def send_zx(step, sub):
         part = core if sub == 0 else 1 - core
@@ -354,6 +357,7 @@
     a_in = [copy_to(own_a, wa.at[0, x], chip(y, (x + d) % NX)) for d in (2, 1, 3)]
     prev = copy_to(x_hbm.at[pl.ds(TOKENS - 16, 16)], prev_buf, at_seq((s + 1) % count))
     send_yb(1)
+    send_xb(0, 1)
     for load in loads:
         load.wait()
     compute()
@@ -377,15 +381,20 @@
     arrived(mate_x)
     send_zx(1, 1)
     send_yb(2)
-    send_xb(0, 3)
-    compute(2)
+    send_xb(1, 2)
+    compute(7)
     send_zx(2, 0)
     send_ya(2, 0)
     send_zx(2, 1)
     send_ya(2, 1)
     send_yb(3)
     send_xb(3, 2)
-    compute(3)
+    compute(4)
+    g_in = []
+    for d in FAR_FIRST:
+        to = (place + d) % ROW
+        g_in.append(copy_to(g_ref.at[to], g_row.at[place], at_seq(y * ROW + to)))
+    g_row[place] = g_ref[place]
     send_zx(3, 0)
     send_ya(3, 0)
     send_zx(3, 1)
@@ -393,33 +402,28 @@
     for side, step in ((1, 3), (-1, 3), (1, 4)):
         arrived(yb[side, step])
     send_xb(5, 3)
-    compute(6)
-
-    g_in = []
-    for d in FAR_FIRST:
-        to = (place + d) % ROW
-        g_in.append(copy_to(g_ref.at[to], g_row.at[place], at_seq(y * ROW + to)))
-    g_row[place] = g_ref[place]
     compute(100)
-    for entry in waiting:
-        if not any(entry is other for other in g_in):
-            arrived(entry)
-    parts = {}
-    for mine in (False, True):
-        block = core if mine else 1 - core
-        for half, weights in enumerate((wa, wb)):
-            total = jnp.zeros((TOKENS, 256), F32)
-            for slot, offset in enumerate(OFFSETS):
-                total = total + dot(xg[row_at(offset), block], weights[slot].reshape(256, 256))
-            if mine:
-                parts[half] = total
-            else:
-                p_send[half] = total
-                parts[half, "copy"] = copy_to(p_send.at[half], p_recv.at[half], mate)
+    row_chain()
+    send_g_col()
+    for entry in list(zx.values()) + list(ya.values()):
+        arrived(entry)
+
+    partial = []
+    for half, weights in enumerate((wa, wb)):
+        if half:
+            for entry in waiting[:-1]:
+                arrived(entry)
+        total = jnp.zeros((2 * TOKENS, 256), F32)
+        for slot, offset in enumerate(OFFSETS):
+            total = total + dot(
+                xg[row_at(offset)].reshape(2 * TOKENS, 256), weights[slot].reshape(256, 256)
+            )
+        p_send[half] = total.reshape(2, TOKENS, 256)
+        partial.append(copy_to(p_send.at[half, 1 - core], p_recv.at[half], mate))
     values = []
     for half in range(2):
-        arrived(parts[half, "copy"])
-        values.append((parts[half] + p_recv[half]).astype(BF16))
+        arrived(partial[half])
+        values.append((p_send[half, core] + p_recv[half]).astype(BF16))
     value = cat(*values, axis=1)
 
     doubled = []
@@ -432,8 +436,6 @@
         to = (place + d) % ROW
         l_in.append(copy_to(l_send.at[to], l_row.at[place], at_seq(y * ROW + to)))
     l_row[place] = l_send[place]
-    row_chain()
-    send_g_col()
     chain = z_chain[...][:, : ROW * HEAD]
     row_total = cat(*split(chain), axis=0)
     for entry in l_in:
@@ -511,7 +513,7 @@
     pltpu.VMEM((NZ, 2, TOKENS, 256), BF16),
     pltpu.VMEM((NY, NX, HEAD, 256), BF16),
     pltpu.VMEM((NY, NX, HEAD, 256), BF16),
-    pltpu.VMEM((2, TOKENS, 256), F32),
+    pltpu.VMEM((2, 2, TOKENS, 256), F32),
     pltpu.VMEM((2, TOKENS, 256), F32),
     pltpu.VMEM((ROW, HEAD, 2 * HEAD), BF16),
     pltpu.VMEM((NY, HEAD, 2 * HEAD), BF16),

time: 58.5 us -> 56.3 us (0.962)
  Pallas kernels: 56.8 us -> 54.5 us
    pallas_call x1, Pallas kernels: 56.8 us -> 54.5 us  [shards(): pl.pallas_call(time_mix, out_shape=jax.ShapeDtypeStruct((TOKENS, WIDTH),...]
where the time goes in v4:
time: 56.3 us; the launch traced here: 56.1 us
  Pallas kernels  54.5 us (97%)
  local copies, waits for them, and re-layouts  1.57 us (3%)
    pallas_call x1, Pallas kernels, shards(): pl.pallas_call(time_mix, out_shape=jax.ShapeDtypeStruct((TOKENS, WIDTH),...  54.5 us
    unnamed x1, local copies, waits for them, and re-layouts  1.57 us

profile of v4, /device:TPU:57, one launch (start us, length us, event | category | flops | bytes accessed | tf_op | source)
XLA Modules:
  0.0 56.1 jit_solution(1464699571983920906)
XLA Ops:
  0.0 54.5 %time_mix.1 = bf16[128,512]{1,0:T(8,128)(2,1)} custom-call(bf16[128,512]{1,0:T(8,128)(2,1)} %x_hbm.1, bf16[64,512]{1,0:T(8,128)(2,1)} %w_ref.1, bf16[128,512]{1,0:T(8,128)(2,1)} %r_hbm.1, bf16[128,512]{1,0:T(8,128)(2,1)} %k_hbm.1, bf16[128,512]{1,0:T(8,128)(2,1)} %a_hbm.1, f32[128,512]{1,0:T(8,128)} %decay_hbm.1, bf16[128,512]{1,0:T(8,128)(2,1)} %gate_hbm.1, ...), custom_call_target="tpu_custom_call" | custom-call | tf_op jit(solution)/shard_map/time_mix/pallas_call | solution.py:554
  54.5 1.6 %copy.13 = bf16[128,512]{1,0:T(8,128)(2,1)} copy(bf16[128,512]{1,0:T(8,128)(2,1)} %time_mix.1) | data formatting | bytes 262144

commit v5 on v4

--- a/solution.py
+++ b/solution.py
@@ -177,7 +177,7 @@
     x_ref, r_ref, k_ref, a_ref, decay_ref, gate_ref,
     y_ref, q_ref, h_ref, g_ref, coef_ref,
     prev_buf, x_send, xg, wa, wb, p_send, p_recv,
-    g_row, g_col, z_chain, z_all, z_row,
+    g_row, g_col, z_chain, z_all, p_all, z_row,
     l_send, l_row, t_send, t_col, s_send, s_in,
     send, recv, local,
 ):
@@ -318,6 +318,7 @@
         chain = (lane == line + ROW * HEAD).astype(F32)
         for j in range(ROW):
             z_all[j] = cat(*split(chain), axis=1)
+            p_all[j] = pack(chain[:, ROW * HEAD : (ROW + 1) * HEAD])
             chain = chain_step(g_row[j], chain) + (lane == line + j * HEAD).astype(F32)
         z_chain[...] = chain
 
@@ -354,8 +355,8 @@
         for _ in range(steps):
             next(stages, None)
 
+    prev = copy_to(x_hbm.at[pl.ds(TOKENS - 16, 16)], prev_buf, at_seq((s + 1) % count))
     a_in = [copy_to(own_a, wa.at[0, x], chip(y, (x + d) % NX)) for d in (2, 1, 3)]
-    prev = copy_to(x_hbm.at[pl.ds(TOKENS - 16, 16)], prev_buf, at_seq((s + 1) % count))
     send_yb(1)
     send_xb(0, 1)
     for load in loads:
@@ -420,17 +421,15 @@
             )
         p_send[half] = total.reshape(2, TOKENS, 256)
         partial.append(copy_to(p_send.at[half, 1 - core], p_recv.at[half], mate))
-    values = []
+    values, doubled = [], []
     for half in range(2):
         arrived(partial[half])
         values.append((p_send[half, core] + p_recv[half]).astype(BF16))
+        for h in range(HEADS // 2 * half, HEADS // 2 * (half + 1)):
+            v = values[half][:, HEAD * (h % 4) : HEAD * (h % 4 + 1)]
+            doubled.append(cat(v, v, axis=0))
+            l_send[h] = pack(dot(h_ref[h], doubled[h]))
     value = cat(*values, axis=1)
-
-    doubled = []
-    for h in range(HEADS):
-        v = value[:, HEAD * h : HEAD * (h + 1)]
-        doubled.append(cat(v, v, axis=0))
-        l_send[h] = pack(dot(h_ref[h], doubled[h]))
     l_in = []
     for d in FAR_FIRST:
         to = (place + d) % ROW
@@ -471,11 +470,9 @@
     entering = fold(dot(z_row[...], t_col[...].reshape(NY * HEAD, 2 * HEAD)))
     entering = pack(entering[:HEAD] + entering[HEAD:])
     twice = cat(entering, entering, axis=0)
+    entered = dot(p_all[...].reshape(ROW * HEAD, 2 * HEAD), twice)
     for j in range(ROW):
-        both = cat(
-            z_all[j, :, wide : wide + HEAD], z_all[j, :, span + wide : span + wide + HEAD], axis=1
-        )
-        s_send[j] = pack(fold(from_row[j] + dot(both, twice)))
+        s_send[j] = pack(fold(from_row[j] + entered[HEAD * j : HEAD * (j + 1)]))
     s_wait = []
     for d in FAR_FIRST:
         to = (place + d) % ROW
@@ -519,6 +516,7 @@
     pltpu.VMEM((NY, HEAD, 2 * HEAD), BF16),
     pltpu.VMEM((HEAD, 640), F32),
     pltpu.VMEM((ROW, HEAD, 2 * 640), BF16),
+    pltpu.VMEM((ROW, HEAD, 2 * HEAD), BF16),
     pltpu.VMEM((2 * HEAD, NY * HEAD), BF16),
     pltpu.VMEM((HEADS, HEAD, 2 * HEAD), BF16),
     pltpu.VMEM((ROW, HEAD, 2 * HEAD), BF16),
@@ -550,7 +548,11 @@
     def row(vector):
         return vector.reshape(1, WIDTH)
 
-    hbm = pl.BlockSpec(memory_space=pl.ANY)
+    hbm = pl.BlockSpec(memory_space=pltpu.HBM)
+
+    def pin(array):
+        return pltpu.with_memory_space_constraint(array, pltpu.HBM)
+
     return pl.pallas_call(
         time_mix,
         out_shape=jax.ShapeDtypeStruct((TOKENS, WIDTH), BF16),
@@ -558,21 +560,21 @@
         out_specs=vmem,
         scratch_shapes=SCRATCH,
         compiler_params=pltpu.CompilerParams(
-            collective_id=0, has_side_effects=True, vmem_limit_bytes=56 << 20
+            collective_id=0, has_side_effects=True, vmem_limit_bytes=48 << 20
         ),
         name="time_mix",
     )(
-        activation_entries,
-        content_mapping_matrix,
-        acceptance_vectors,
-        address_vectors_given,
-        inline_adaptation_speed,
-        memory_fading_factors,
-        result_filter_given,
-        row(content_lagged_blend),
-        row(extra_coordinate_factors),
-        row(group_layernorm_scaling),
-        row(group_layernorm_offset),
+        pin(activation_entries),
+        pin(content_mapping_matrix),
+        pin(acceptance_vectors),
+        pin(address_vectors_given),
+        pin(inline_adaptation_speed),
+        pin(memory_fading_factors),
+        pin(result_filter_given),
+        pin(row(content_lagged_blend)),
+        pin(row(extra_coordinate_factors)),
+        pin(row(group_layernorm_scaling)),
+        pin(row(group_layernorm_offset)),
     )
 
 

time: 56.3 us -> 54.8 us (0.973)
  local copies, waits for them, and re-layouts: 1.57 us -> 0.66 us
  Pallas kernels: 54.5 us -> 53.9 us
    unnamed x1, local copies, waits for them, and re-layouts: 1.57 us -> 0.66 us
    pallas_call x1, Pallas kernels: 54.5 us -> 53.9 us  [shards(): pl.pallas_call(time_mix, out_shape=jax.ShapeDtypeStruct((TOKENS, WIDTH),...]
where the time goes in v5:
time: 54.8 us; the launch traced here: 54.6 us
  Pallas kernels  53.9 us (98%)
  local copies, waits for them, and re-layouts  0.66 us (1%)
    pallas_call x1, Pallas kernels, shards(): pl.pallas_call(time_mix, out_shape=jax.ShapeDtypeStruct((TOKENS, WIDTH),...  53.9 us

profile of v5, /device:TPU:57, one launch (start us, length us, event | category | flops | bytes accessed | tf_op | source)
XLA Modules:
  0.0 54.6 jit_solution(14942607043012625708)
XLA Ops:
  0.0 53.9 %time_mix.1 = bf16[128,512]{1,0:T(8,128)(2,1)S(1)} custom-call(bf16[128,512]{1,0:T(8,128)(2,1)} %x_hbm.1, bf16[64,512]{1,0:T(8,128)(2,1)} %w_ref.1, bf16[128,512]{1,0:T(8,128)(2,1)} %r_hbm.1, bf16[128,512]{1,0:T(8,128)(2,1)} %k_hbm.1, bf16[128,512]{1,0:T(8,128)(2,1)} %a_hbm.1, f32[128,512]{1,0:T(8,128)} %decay_hbm.1, bf16[128,512]{1,0:T(8,128)(2,1)} %gate_hbm.1, ...), custom_call_target="tpu_custom_call" | custom-call | tf_op jit(solution)/shard_map/time_mix/pallas_call | solution.py:556
  54.0 0.7 %copy.13 = bf16[128,512]{1,0:T(8,128)(2,1)} copy(bf16[128,512]{1,0:T(8,128)(2,1)S(1)} %time_mix.1) | data formatting | bytes 262144

commit v6 on v5

--- a/solution.py
+++ b/solution.py
@@ -361,7 +361,6 @@
     send_xb(0, 1)
     for load in loads:
         load.wait()
-    compute()
 
     arrived(prev)
     own = x_ref[...].astype(F32)
@@ -383,7 +382,7 @@
     send_zx(1, 1)
     send_yb(2)
     send_xb(1, 2)
-    compute(7)
+    compute(8)
     send_zx(2, 0)
     send_ya(2, 0)
     send_zx(2, 1)

time: 54.8 us -> 54.2 us (0.989)
  no operation moved by 1% of the time
where the time goes in v6:
time: 54.2 us; the launch traced here: 54.1 us
  Pallas kernels  53.4 us (99%)
  local copies, waits for them, and re-layouts  0.66 us (1%)
    pallas_call x1, Pallas kernels, shards(): pl.pallas_call(time_mix, out_shape=jax.ShapeDtypeStruct((TOKENS, WIDTH),...  53.4 us

profile of v6, /device:TPU:57, one launch (start us, length us, event | category | flops | bytes accessed | tf_op | source)
XLA Modules:
  0.0 54.1 jit_solution(17472287950318337469)
XLA Ops:
  0.0 53.4 %time_mix.1 = bf16[128,512]{1,0:T(8,128)(2,1)S(1)} custom-call(bf16[128,512]{1,0:T(8,128)(2,1)} %x_hbm.1, bf16[64,512]{1,0:T(8,128)(2,1)} %w_ref.1, bf16[128,512]{1,0:T(8,128)(2,1)} %r_hbm.1, bf16[128,512]{1,0:T(8,128)(2,1)} %k_hbm.1, bf16[128,512]{1,0:T(8,128)(2,1)} %a_hbm.1, f32[128,512]{1,0:T(8,128)} %decay_hbm.1, bf16[128,512]{1,0:T(8,128)(2,1)} %gate_hbm.1, ...), custom_call_target="tpu_custom_call" | custom-call | tf_op jit(solution)/shard_map/time_mix/pallas_call | solution.py:555
  53.4 0.7 %copy.13 = bf16[128,512]{1,0:T(8,128)(2,1)} copy(bf16[128,512]{1,0:T(8,128)(2,1)S(1)} %time_mix.1) | data formatting | bytes 262144

commit v7 on v6

--- a/solution.py
+++ b/solution.py
@@ -434,6 +434,7 @@
         to = (place + d) % ROW
         l_in.append(copy_to(l_send.at[to], l_row.at[place], at_seq(y * ROW + to)))
     l_row[place] = l_send[place]
+    column_chain()
     chain = z_chain[...][:, : ROW * HEAD]
     row_total = cat(*split(chain), axis=0)
     for entry in l_in:
@@ -464,7 +465,6 @@
     extra = coef_ref[...] * value.astype(F32)
     gate = gate_ref[...].astype(F32)
 
-    column_chain()
     arrived_from_below()
     entering = fold(dot(z_row[...], t_col[...].reshape(NY * HEAD, 2 * HEAD)))
     entering = pack(entering[:HEAD] + entering[HEAD:])

time: 54.2 us -> 54.2 us (level)
  no operation moved by 1% of the time
where the time goes in v7:
time: 54.2 us; the launch traced here: 54.1 us
  Pallas kernels  53.4 us (99%)
  local copies, waits for them, and re-layouts  0.66 us (1%)
    pallas_call x1, Pallas kernels, shards(): pl.pallas_call(time_mix, out_shape=jax.ShapeDtypeStruct((TOKENS, WIDTH),...  53.4 us

profile of v7, /device:TPU:57, one launch (start us, length us, event | category | flops | bytes accessed | tf_op | source)
XLA Modules:
  0.0 54.1 jit_solution(16698895571166897559)
XLA Ops:
  0.0 53.4 %time_mix.1 = bf16[128,512]{1,0:T(8,128)(2,1)S(1)} custom-call(bf16[128,512]{1,0:T(8,128)(2,1)} %x_hbm.1, bf16[64,512]{1,0:T(8,128)(2,1)} %w_ref.1, bf16[128,512]{1,0:T(8,128)(2,1)} %r_hbm.1, bf16[128,512]{1,0:T(8,128)(2,1)} %k_hbm.1, bf16[128,512]{1,0:T(8,128)(2,1)} %a_hbm.1, f32[128,512]{1,0:T(8,128)} %decay_hbm.1, bf16[128,512]{1,0:T(8,128)(2,1)} %gate_hbm.1, ...), custom_call_target="tpu_custom_call" | custom-call | tf_op jit(solution)/shard_map/time_mix/pallas_call | solution.py:555
  53.4 0.7 %copy.13 = bf16[128,512]{1,0:T(8,128)(2,1)} copy(bf16[128,512]{1,0:T(8,128)(2,1)S(1)} %time_mix.1) | data formatting | bytes 262144
